TPU v7x, 32 devices: a whole 2x2x4 slice. The times are simulated.
32 devices in a mesh: rows: 8 (over y, x, core), cols: 4 (over z).
Axes of the slice: x: 2, y: 2, z: 4, core: 2. Of those that a mesh axis runs over, the one named last changes fastest.
Arguments:
- field_real: float32 [6144, 6144], P('rows', 'cols'), may hold values from -6 to 6
- field_imag: float32 [6144, 6144], P('rows', 'cols'), may hold values from -6 to 6
- kerr_map: float32 [6144, 6144], P('rows', 'cols'), may hold values from 0.1 to 1
- pinhole: int32 [6144, 6144], P(None, ('rows', 'cols')), may hold values from 0 to 1, as said below
Outputs:
- out_real: float32 [6144, 6144], P('rows', 'cols')
- out_imag: float32 [6144, 6144], P('rows', 'cols')
- b_integral: float32 [6144, 6144], P('rows', 'cols')
Inputs may be any that keep to these rules, and one draw needn't show every extreme that they name: pinhole is 1 at every far-field pixel whose frequency (indices above 3072 taken as negative, so the disc wraps to the corners) lies inside a disc about zero frequency of radius R, and 0 outside it, except within about two pixels of the disc's rim, where it may take either value; R lies between 1536 and 2048 and varies from draw to draw.
All inputs are finite; a program needn't handle non-finite values.
Results may differ from a plain program's by a relative error of at most 0.00014.
Values sent between devices are 32-bit elements; how exact they have to be, the bound alone decides.
A program may use at most 192 MiB of HBM per device.

v0:
```python
import math

import jax
import jax.numpy as jnp
from jax import lax
from jax.sharding import PartitionSpec as P

RADIX = 128


def phase_pair(first, second, period):
    product = first[:, None] * second[None, :] % period
    angle = 2.0 * math.pi / period * product.astype(jnp.float32)
    return (jnp.cos(angle), jnp.sin(angle))


def complex_apply(form, real_part, imag_part, cos_table, sin_table, backward, precision):
    weight = 1.0 if backward else -1.0
    real_cos = jnp.einsum(form, real_part, cos_table, precision=precision)
    real_sin = jnp.einsum(form, real_part, sin_table, precision=precision)
    imag_cos = jnp.einsum(form, imag_part, cos_table, precision=precision)
    imag_sin = jnp.einsum(form, imag_part, sin_table, precision=precision)
    return (real_cos - weight * imag_sin, imag_cos + weight * real_sin)


def twiddle(real_part, imag_part, cos_table, sin_table, backward):
    weight = 1.0 if backward else -1.0
    return (
        real_part * cos_table - weight * imag_part * sin_table,
        imag_part * cos_table + weight * real_part * sin_table,
    )


def transform_last(real_part, imag_part, backward):
    rows_here, length = real_part.shape
    blocks = length // RADIX
    outer = jnp.arange(blocks, dtype=jnp.int32)
    inner = jnp.arange(RADIX, dtype=jnp.int32)
    real_part = real_part.reshape(rows_here, blocks, RADIX)
    imag_part = imag_part.reshape(rows_here, blocks, RADIX)
    cos_outer, sin_outer = phase_pair(outer, outer, blocks)
    real_part, imag_part = complex_apply(
        "mab,ak->mkb", real_part, imag_part, cos_outer, sin_outer, backward, lax.Precision.HIGH
    )
    cos_mid, sin_mid = phase_pair(outer, inner, length)
    real_part, imag_part = twiddle(real_part, imag_part, cos_mid, sin_mid, backward)
    cos_inner, sin_inner = phase_pair(inner, inner, RADIX)
    real_part, imag_part = complex_apply(
        "mkb,bj->mkj", real_part, imag_part, cos_inner, sin_inner, backward, lax.Precision.HIGH
    )
    scale = 1.0 / math.sqrt(length)
    real_part = jnp.transpose(real_part, (0, 2, 1)).reshape(rows_here, length) * scale
    imag_part = jnp.transpose(imag_part, (0, 2, 1)).reshape(rows_here, length) * scale
    return (real_part, imag_part)


def kerr_phase(real_part, imag_part, kerr_part):
    power = real_part * real_part + imag_part * imag_part
    phase = kerr_part * power
    cosine = jnp.cos(phase)
    sine = jnp.sin(phase)
    return (real_part * cosine - imag_part * sine, real_part * sine + imag_part * cosine, phase)


def to_tall(real_part, imag_part):
    rows_here, length = real_part.shape
    device_count = lax.axis_size(("rows", "cols"))
    each = length // device_count
    real_part = real_part.reshape(rows_here, device_count, each)
    imag_part = imag_part.reshape(rows_here, device_count, each)
    real_part, imag_part = (
        lax.all_to_all(real_part, ("rows", "cols"), split_axis=1, concat_axis=0, tiled=True),
        lax.all_to_all(imag_part, ("rows", "cols"), split_axis=1, concat_axis=0, tiled=True),
    )
    real_part = jnp.transpose(real_part.reshape(device_count, rows_here, each), (2, 0, 1))
    imag_part = jnp.transpose(imag_part.reshape(device_count, rows_here, each), (2, 0, 1))
    return (real_part.reshape(each, length), imag_part.reshape(each, length))


def from_tall(real_part, imag_part):
    each, length = real_part.shape
    device_count = lax.axis_size(("rows", "cols"))
    rows_here = length // device_count
    real_part = jnp.transpose(real_part.reshape(each, device_count, rows_here), (1, 2, 0))
    imag_part = jnp.transpose(imag_part.reshape(each, device_count, rows_here), (1, 2, 0))
    real_part, imag_part = (
        lax.all_to_all(real_part, ("rows", "cols"), split_axis=0, concat_axis=2, tiled=True),
        lax.all_to_all(imag_part, ("rows", "cols"), split_axis=0, concat_axis=2, tiled=True),
    )
    return (real_part.reshape(rows_here, length), imag_part.reshape(rows_here, length))


def chirp_line(index, length):
    square = index * index % (2 * length)
    angle = -(math.pi / length) * square.astype(jnp.float32)
    return (jnp.cos(angle), jnp.sin(angle))


def multiply(real_part, imag_part, other_real, other_imag):
    return (
        real_part * other_real - imag_part * other_imag,
        real_part * other_imag + imag_part * other_real,
    )


def spectral_pair(real_part, imag_part, table_real, table_imag, backward, precision):
    rows_here, length = real_part.shape
    blocks = length // RADIX
    outer = jnp.arange(blocks, dtype=jnp.int32)
    inner = jnp.arange(RADIX, dtype=jnp.int32)
    real_part = real_part.reshape(rows_here, blocks, RADIX)
    imag_part = imag_part.reshape(rows_here, blocks, RADIX)
    cos_outer, sin_outer = phase_pair(outer, outer, blocks)
    cos_mid, sin_mid = phase_pair(outer, inner, length)
    cos_inner, sin_inner = phase_pair(inner, inner, RADIX)
    real_part, imag_part = complex_apply(
        "mab,ak->mkb", real_part, imag_part, cos_outer, sin_outer, False, precision
    )
    real_part, imag_part = twiddle(real_part, imag_part, cos_mid, sin_mid, False)
    real_part, imag_part = complex_apply(
        "mkb,bj->mkj", real_part, imag_part, cos_inner, sin_inner, False, precision
    )
    real_part, imag_part = multiply(real_part, imag_part, table_real, table_imag)
    real_part, imag_part = complex_apply(
        "mkj,jb->mkb", real_part, imag_part, cos_inner, sin_inner, backward, precision
    )
    real_part, imag_part = twiddle(real_part, imag_part, cos_mid, sin_mid, backward)
    real_part, imag_part = complex_apply(
        "mkb,ka->mab", real_part, imag_part, cos_outer, sin_outer, backward, precision
    )
    return (real_part.reshape(rows_here, length), imag_part.reshape(rows_here, length))


def tile_to_columns(part):
    wide = lax.all_to_all(part, "rows", split_axis=1, concat_axis=0, tiled=True)
    return jnp.transpose(wide)


def columns_to_rows(real_part, imag_part):
    each, length = real_part.shape
    row_count, col_count = lax.axis_size("rows"), lax.axis_size("cols")
    device_count = row_count * col_count
    rows_here = length // device_count

    def send(part):
        part = part.reshape(each, row_count, col_count, rows_here)
        part = jnp.transpose(part, (2, 1, 3, 0)).reshape(device_count, rows_here, each)
        part = lax.all_to_all(part, ("cols", "rows"), split_axis=0, concat_axis=2, tiled=True)
        return part.reshape(rows_here, length)

    return (send(real_part), send(imag_part))


def per_device(field_real, field_imag, kerr_map, pinhole):
    real_part, imag_part, phase_one = kerr_phase(field_real, field_imag, kerr_map)
    real_part, imag_part = tile_to_columns(real_part), tile_to_columns(imag_part)
    kerr_wide = lax.all_to_all(kerr_map, "cols", split_axis=0, concat_axis=1, tiled=True)
    length, each = pinhole.shape
    blocks = length // RADIX
    scale = 1.0 / length
    split_index = (
        jnp.arange(blocks, dtype=jnp.int32)[:, None]
        + blocks * jnp.arange(RADIX, dtype=jnp.int32)[None, :]
    )
    line_cos, line_sin = chirp_line(split_index, length)
    line_cos, line_sin = line_cos * scale, line_sin * scale
    own = lax.axis_index(("rows", "cols")) * each + jnp.arange(each, dtype=jnp.int32)
    own_cos, own_sin = chirp_line(own, length)
    own_cos, own_sin = own_cos[:, None, None], own_sin[:, None, None]
    aperture = jnp.transpose(pinhole.reshape(RADIX, blocks, each), (2, 1, 0)).astype(jnp.float32)
    table_real, table_imag = multiply(line_cos[None], line_sin[None], own_cos, own_sin)
    table_real, table_imag = table_real * aperture, table_imag * aperture
    real_part, imag_part = spectral_pair(real_part, imag_part, line_cos, line_sin, True, lax.Precision.HIGHEST)
    real_part, imag_part = columns_to_rows(real_part, imag_part)
    real_part, imag_part = spectral_pair(real_part, imag_part, line_cos, line_sin, True, lax.Precision.HIGHEST)
    real_part, imag_part, phase_two = kerr_phase(real_part, imag_part, kerr_wide)
    phase_back = lax.all_to_all(phase_two, "cols", split_axis=1, concat_axis=0, tiled=True)
    real_part, imag_part = transform_last(real_part, imag_part, False)
    real_part, imag_part = to_tall(real_part, imag_part)
    real_part, imag_part = spectral_pair(real_part, imag_part, table_real, table_imag, False, lax.Precision.HIGH)
    real_part, imag_part = from_tall(real_part, imag_part)
    real_part, imag_part = transform_last(real_part, imag_part, False)
    out_real, out_imag = (
        lax.all_to_all(real_part, "cols", split_axis=1, concat_axis=0, tiled=True),
        lax.all_to_all(imag_part, "cols", split_axis=1, concat_axis=0, tiled=True),
    )
    return (out_real, out_imag, phase_one + phase_back)


def solution(mesh):
    placed = (P("rows", "cols"), P("rows", "cols"), P("rows", "cols"), P(None, ("rows", "cols")))
    return jax.shard_map(
        per_device,
        mesh=mesh,
        in_specs=placed,
        out_specs=(P("rows", "cols"), P("rows", "cols"), P("rows", "cols")),
        check_vma=False,
    )
```

profile of v0, /device:TPU:0, one launch (start us, length us, event | category | flops | bytes accessed | tf_op | source)
XLA Modules:
  0.0 1752.6 jit_solution(3592784836356387675)
XLA Ops:
  18.8 17.2 fusion.568
  36.1 17.1 multiply_add_fusion.20
  53.2 59.7 %all_to_all.195 = f32[768,8,192]{0,2,1:T(8,128)} all-to-all(f32[768,8,192]{0,2,1:T(8,128)S(1)} %bitcast.406), channel_id=1, replica_groups=mesh['rows'=8,'cols'=4] {'rows'}, dimensions={1} | all-to-all | bytes 9437184 | tf_op jit(solution)/shard_map/all_to_all | solution.py:135
  129.7 42.6 %all-to-all-done.1 = f32[768,8,192]{0,2,1:T(8,128)} async-done(((f32[768,8,192]{0,2,1:T(8,128)}), f32[768,8,192]{0,2,1:T(8,128)}, u32[]{:S(2)}, u32[]{:S(2)}) %all-to-all-start.1) | async-done | bytes 4718624 | tf_op jit(solution)/shard_map/all_to_all | solution.py:135
  260.0 19.1 %all-to-all-done.4 = f32[4,192,1536]{2,1,0:T(8,128)} async-done(((f32[4,192,1536]{2,1,0:T(8,128)}), f32[4,192,1536]{2,1,0:T(8,128)}, u32[]{:S(2)}, u32[]{:S(2)}) %all-to-all-start.4) | async-done | bytes 4718624 | tf_op jit(solution)/shard_map/all_to_all | solution.py:157
  292.6 9.0 add_bitcast_fusion.1
  318.2 106.2 %all-to-all-done.2 = f32[32,192,192]{2,1,0:T(8,128)} async-done(((f32[32,192,192]{2,1,0:T(8,128)}), f32[32,192,192]{2,1,0:T(8,128)}, u32[]{:S(2)}, u32[]{:S(2)}) %all-to-all-start.2) | async-done | bytes 4718624 | tf_op jit(solution)/shard_map/all_to_all | solution.py:148
  442.2 9.1 copy.82
  467.8 100.2 %all-to-all-done.3 = f32[32,192,192]{2,1,0:T(8,128)} async-done(((f32[32,192,192]{2,1,0:T(8,128)}), f32[32,192,192]{2,1,0:T(8,128)}, u32[]{:S(2)}, u32[]{:S(2)}) %all-to-all-start.3) | async-done | bytes 4718624 | tf_op jit(solution)/shard_map/all_to_all | solution.py:148
  567.9 9.1 copy.84
  663.5 19.3 %fusion.181 = f32[48,192,128]{2,0,1:T(8,128)S(1)} fusion(f32[48,192,128]{2,0,1:T(8,128)S(1)} %get-tuple-element.21, f32[48,192,128]{2,0,1:T(8,128)S(1)} %convolution_subtract_fusion, f32[192,48,128]{2,1,0:T(8,128)S(1)} %bitcast.375), kind=kOutput, calls=%fused_computation.205 | convolution fusion | flops 348016896 | bytes 18874368 | tf_op jit(solution)/shard_map/mab,ak->mkb/dot_general | solution.py:19
  682.7 19.6 %fusion.179 = f32[48,192,128]{2,0,1:T(8,128)S(1)} fusion(f32[48,192,128]{2,0,1:T(8,128)S(1)} %get-tuple-element.21, f32[48,192,128]{2,0,1:T(8,128)S(1)} %convolution_subtract_fusion, f32[192,48,128]{2,1,0:T(8,128)S(1)} %bitcast.375), kind=kOutput, calls=%fused_computation.203 | convolution fusion | flops 348016896 | bytes 18874368 | tf_op jit(solution)/shard_map/mab,ak->mkb/dot_general | solution.py:21
  702.4 19.9 %multiply_subtract_fusion.9 = f32[48,192,128]{2,0,1:T(8,128)S(1)} fusion(f32[48,192,128]{2,0,1:T(8,128)S(1)} %fusion.181, f32[48,192,128]{2,0,1:T(8,128)S(1)} %get-tuple-element.21, f32[48,192,128]{2,0,1:T(8,128)S(1)} %convolution_subtract_fusion, f32[192,48,128]{2,1,0:T(8,128)S(1)} %bitcast.375), kind=kOutput, calls=%fused_computation.79 | convolution fusion | flops 350376192 | bytes 23592960 | tf_op jit(solution)/shard_map/mab,ak->mkb/dot_general | solution.py:22
  722.3 20.0 %multiply_add_fusion.9 = f32[48,192,128]{2,0,1:T(8,128)S(1)} fusion(f32[48,192,128]{2,0,1:T(8,128)S(1)} %fusion.179, f32[48,192,128]{2,0,1:T(8,128)S(1)} %get-tuple-element.21, f32[48,192,128]{2,0,1:T(8,128)S(1)} %convolution_subtract_fusion, f32[192,48,128]{2,1,0:T(8,128)S(1)} %bitcast.375), kind=kOutput, calls=%fused_computation.78 | convolution fusion | flops 350376192 | bytes 23592960 | tf_op jit(solution)/shard_map/mab,ak->mkb/dot_general | solution.py:20
  779.7 116.8 %all-to-all-done.5 = f32[192,32,192]{0,2,1:T(8,128)} async-done(((f32[192,32,192]{0,2,1:T(8,128)}), f32[192,32,192]{0,2,1:T(8,128)}, u32[]{:S(2)}, u32[]{:S(2)}) %all-to-all-start.5) | async-done | bytes 4718624 | tf_op jit(solution)/shard_map/all_to_all | solution.py:72
  921.7 9.1 copy.87
  945.3 95.3 %all-to-all-done.6 = f32[192,32,192]{0,2,1:T(8,128)} async-done(((f32[192,32,192]{0,2,1:T(8,128)}), f32[192,32,192]{0,2,1:T(8,128)}, u32[]{:S(2)}, u32[]{:S(2)}) %all-to-all-start.6) | async-done | bytes 4718624 | tf_op jit(solution)/shard_map/all_to_all | solution.py:73
  1040.6 9.1 copy.89
  1114.5 9.2 copy.113
  1160.3 107.2 %all-to-all-done.7 = f32[32,192,192]{1,2,0:T(8,128)} async-done(((f32[32,192,192]{1,2,0:T(8,128)}), f32[32,192,192]{1,2,0:T(8,128)}, u32[]{:S(2)}, u32[]{:S(2)}) %all-to-all-start.7) | async-done | bytes 4718624 | tf_op jit(solution)/shard_map/all_to_all | solution.py:87
  1288.5 122.9 %all-to-all-done.8 = f32[32,192,192]{1,2,0:T(8,128)} async-done(((f32[32,192,192]{1,2,0:T(8,128)}), f32[32,192,192]{1,2,0:T(8,128)}, u32[]{:S(2)}, u32[]{:S(2)}) %all-to-all-start.8) | async-done | bytes 4718624 | tf_op jit(solution)/shard_map/all_to_all | solution.py:88
  1462.6 60.8 %all-to-all-done.11 = f32[192,4,1536]{2,0,1:T(8,128)} async-done(((f32[192,4,1536]{2,0,1:T(8,128)}), f32[192,4,1536]{2,0,1:T(8,128)}, u32[]{:S(2)}, u32[]{:S(2)}) %all-to-all-start.11) | async-done | bytes 4718624 | tf_op jit(solution)/shard_map/all_to_all | solution.py:177
  1554.6 79.0 %all-to-all-done.9 = f32[192,4,1536]{2,0,1:T(8,128)} async-done(((f32[192,4,1536]{2,0,1:T(8,128)}), f32[192,4,1536]{2,0,1:T(8,128)}, u32[]{:S(2)}, u32[]{:S(2)}) %all-to-all-start.9) | async-done | bytes 4718624 | tf_op jit(solution)/shard_map/all_to_all | solution.py:184
  1657.2 85.5 %all-to-all-done.10 = f32[192,4,1536]{2,0,1:T(8,128)} async-done(((f32[192,4,1536]{2,0,1:T(8,128)}), f32[192,4,1536]{2,0,1:T(8,128)}, u32[]{:S(2)}, u32[]{:S(2)}) %all-to-all-start.10) | async-done | bytes 4718624 | tf_op jit(solution)/shard_map/all_to_all | solution.py:185
  (195 shorter events, 587.5 us)
Async XLA Ops:
  12.7 23.3 %slice-start.16 = ((s8[4718592]{0:T(1024)(128)(4,1)}), s8[524288]{0:T(1024)(128)(4,1)S(1)}, s32[]{:S(2)}) async-start(s8[4718592]{0:T(1024)(128)(4,1)} %bitcast.390), calls=%async_computation.28 | async-start | bytes 1048576
  18.8 17.2 slice-start.17
  18.8 17.2 copy-start.10
  36.0 17.2 copy-start.8
  113.0 59.3 %all-to-all-start.1 = ((f32[768,8,192]{0,2,1:T(8,128)}), f32[768,8,192]{0,2,1:T(8,128)}, u32[]{:S(2)}, u32[]{:S(2)}) async-start(f32[768,8,192]{0,2,1:T(8,128)} %bitcast.403), calls=%async_computation.1 | async-start | bytes 9437184 | tf_op jit(solution)/shard_map/all_to_all | solution.py:135
  172.3 106.9 %all-to-all-start.4 = ((f32[4,192,1536]{2,1,0:T(8,128)}), f32[4,192,1536]{2,1,0:T(8,128)}, u32[]{:S(2)}, u32[]{:S(2)}) async-start(f32[4,192,1536]{2,1,0:T(8,128)} %bitcast.407), calls=%async_computation.4 | async-start | bytes 9437184 | tf_op jit(solution)/shard_map/all_to_all | solution.py:157
  180.6 10.3 slice-start.10
  279.2 13.4 slice-start.6
  279.2 145.2 %all-to-all-start.2 = ((f32[32,192,192]{2,1,0:T(8,128)}), f32[32,192,192]{2,1,0:T(8,128)}, u32[]{:S(2)}, u32[]{:S(2)}) async-start(f32[32,192,192]{2,1,0:T(8,128)} %bitcast.394), calls=%async_computation.2 | async-start | bytes 12582912 | tf_op jit(solution)/shard_map/all_to_all | solution.py:148
  424.4 143.5 %all-to-all-start.3 = ((f32[32,192,192]{2,1,0:T(8,128)}), f32[32,192,192]{2,1,0:T(8,128)}, u32[]{:S(2)}, u32[]{:S(2)}) async-start(f32[32,192,192]{2,1,0:T(8,128)} %bitcast.395), calls=%async_computation.3 | async-start | bytes 12582912 | tf_op jit(solution)/shard_map/all_to_all | solution.py:148
  584.5 13.3 slice-start.12
  650.0 13.5 slice-start.4
  722.3 22.5 %copy-start.6 = (f32[48,192,128]{2,0,1:T(8,128)}, f32[48,192,128]{2,0,1:T(8,128)S(1)}, u32[]{:S(2)}) copy-start(f32[48,192,128]{2,0,1:T(8,128)S(1)} %multiply_subtract_fusion.9) | copy-start | bytes 14155780
  756.1 9.8 slice-start.8
  756.1 140.5 %all-to-all-start.5 = ((f32[192,32,192]{0,2,1:T(8,128)}), f32[192,32,192]{0,2,1:T(8,128)}, u32[]{:S(2)}, u32[]{:S(2)}) async-start(f32[192,32,192]{0,2,1:T(8,128)} %bitcast.399), calls=%async_computation.5 | async-start | bytes 12582912 | tf_op jit(solution)/shard_map/all_to_all | solution.py:72
  896.6 144.0 %all-to-all-start.6 = ((f32[192,32,192]{0,2,1:T(8,128)}), f32[192,32,192]{0,2,1:T(8,128)}, u32[]{:S(2)}, u32[]{:S(2)}) async-start(f32[192,32,192]{0,2,1:T(8,128)} %bitcast.398), calls=%async_computation.6 | async-start | bytes 12582912 | tf_op jit(solution)/shard_map/all_to_all | solution.py:73
  1057.6 9.9 slice-start.14
  1123.7 13.4 slice-start.2
  1123.7 143.8 %all-to-all-start.7 = ((f32[32,192,192]{1,2,0:T(8,128)}), f32[32,192,192]{1,2,0:T(8,128)}, u32[]{:S(2)}, u32[]{:S(2)}) async-start(f32[32,192,192]{1,2,0:T(8,128)} %bitcast.397), calls=%async_computation.7 | async-start | bytes 12582912 | tf_op jit(solution)/shard_map/all_to_all | solution.py:87
  1267.5 143.8 %all-to-all-start.8 = ((f32[32,192,192]{1,2,0:T(8,128)}), f32[32,192,192]{1,2,0:T(8,128)}, u32[]{:S(2)}, u32[]{:S(2)}) async-start(f32[32,192,192]{1,2,0:T(8,128)} %bitcast.396), calls=%async_computation.8 | async-start | bytes 12582912 | tf_op jit(solution)/shard_map/all_to_all | solution.py:88
  1411.3 112.0 %all-to-all-start.11 = ((f32[192,4,1536]{2,0,1:T(8,128)}), f32[192,4,1536]{2,0,1:T(8,128)}, u32[]{:S(2)}, u32[]{:S(2)}) async-start(f32[192,4,1536]{2,0,1:T(8,128)} %copy_multiply_fusion), calls=%async_computation.11 | async-start | bytes 9437184 | tf_op jit(solution)/shard_map/all_to_all | solution.py:177
  1523.4 11.2 slice-start
  1523.4 110.2 %all-to-all-start.9 = ((f32[192,4,1536]{2,0,1:T(8,128)}), f32[192,4,1536]{2,0,1:T(8,128)}, u32[]{:S(2)}, u32[]{:S(2)}) async-start(f32[192,4,1536]{2,0,1:T(8,128)} %copy.97), calls=%async_computation.9 | async-start | bytes 9437184 | tf_op jit(solution)/shard_map/all_to_all | solution.py:184
  1633.6 109.1 %all-to-all-start.10 = ((f32[192,4,1536]{2,0,1:T(8,128)}), f32[192,4,1536]{2,0,1:T(8,128)}, u32[]{:S(2)}, u32[]{:S(2)}) async-start(f32[192,4,1536]{2,0,1:T(8,128)} %copy.99), calls=%async_computation.10 | async-start | bytes 9437184 | tf_op jit(solution)/shard_map/all_to_all | solution.py:185
  (23 other events, 127.8 us)
where the time goes:
time: 1760 us; the launch traced here: 1750 us
  waiting for transfers between devices  936 us (53%)
  matrix products  374 us (21%)
  local copies, waits for them, and re-layouts  267 us (15%)
  starting transfers between devices  60.1 us (3%)
  blocking collectives  59.7 us (3%)
  other arithmetic  53.9 us (3%)
    all_to_all x2, waiting for transfers between devices, send(): lax.all_to_all(part, ('cols', 'rows'), split_axis=0, concat_axis=2, tiled...  206 us
    all_to_all x1, waiting for transfers between devices, from_tall(): lax.all_to_all(imag_part, ('rows', 'cols'), split_axis=0, concat_axis=2,...  123 us
    all_to_all x1, waiting for transfers between devices, to_tall(): lax.all_to_all(real_part, ('rows', 'cols'), split_axis=1, concat_axis=0,...  117 us
    all_to_all x1, waiting for transfers between devices, from_tall(): lax.all_to_all(real_part, ('rows', 'cols'), split_axis=0, concat_axis=2,...  107 us
    dot_general x16, matrix products, complex_apply(): real_sin = jnp.einsum(form, real_part, sin_table, precision=precision)  104 us
    all_to_all x1, waiting for transfers between devices, to_tall(): lax.all_to_all(imag_part, ('rows', 'cols'), split_axis=1, concat_axis=0,...  95.3 us
    dot_general x16, matrix products, complex_apply(): imag_cos = jnp.einsum(form, imag_part, cos_table, precision=precision)  94.9 us
    dot_general x16, matrix products, complex_apply(): real_cos = jnp.einsum(form, real_part, cos_table, precision=precision)  90.6 us
  transfers between devices with their start and end apart: 11, of which 11 were waited for; matrix products, arithmetic and copies ran while one was open for 20% of the time, Pallas kernels for 0%

commit v1 on v0

--- a/solution.py
+++ b/solution.py
@@ -1,8 +1,12 @@
+import functools
 import math
 
 import jax
 import jax.numpy as jnp
+import numpy as np
 from jax import lax
+from jax.experimental import pallas as pl
+from jax.experimental.pallas import tpu as pltpu
 from jax.sharding import PartitionSpec as P
 
 RADIX = 128
@@ -187,10 +191,588 @@
     return (out_real, out_imag, phase_one + phase_back)
 
 
+LANES = 128
+
+
+def as_pair(values):
+    high = values.astype(np.float32).astype(jnp.bfloat16)
+    low = (values - high.astype(np.float64)).astype(np.float32).astype(jnp.bfloat16)
+    return np.stack([high, low])
+
+
+def phase_of(product, period):
+    return 2.0 * np.pi * (product % period) / period
+
+
+def rows_matrix(angle, scale):
+    return as_pair(np.concatenate([np.cos(angle), np.sin(angle)], axis=0) * scale)
+
+
+def packed(values, tail_width=64):
+    half = values.shape[-1] - LANES
+    pad = [(0, 0)] * (values.ndim - 1) + [(0, tail_width - half)]
+    return values[..., :LANES], np.pad(values[..., LANES:], pad)
+
+
+def packed_columns(real_rows, imag_rows):
+    real_main, real_tail = packed(real_rows)
+    imag_main, imag_tail = packed(imag_rows)
+    return np.concatenate([real_main, imag_main, real_tail, imag_tail], axis=-1)
+
+
+def transposed_matrix(angle, scale):
+    cosine, sine = np.cos(angle) * scale, np.sin(angle) * scale
+    upper = packed_columns(cosine, sine)
+    lower = packed_columns(-sine, cosine)
+    return as_pair(np.concatenate([upper, lower], axis=0))
+
+
+def lane_square(angle_in_out, scale):
+    cosine, sine = np.cos(angle_in_out) * scale, np.sin(angle_in_out) * scale
+    from_real = packed_columns(cosine, -sine)
+    from_imag = packed_columns(sine, cosine)
+    rows = from_real.shape[0]
+    pad = np.zeros((64 - (rows - LANES), from_real.shape[1]))
+    return as_pair(np.concatenate(
+        [from_real[:LANES], from_imag[:LANES], from_real[LANES:], pad, from_imag[LANES:], pad], axis=0
+    ))
+
+
+def lane_table(angle):
+    cosine, sine = np.cos(angle), -np.sin(angle)
+    cos_main, cos_tail = packed(cosine)
+    sin_main, sin_tail = packed(sine)
+    return np.stack([
+        cos_main, sin_main,
+        np.concatenate([cos_tail, cos_tail], axis=-1),
+        np.concatenate([-sin_tail, sin_tail], axis=-1),
+    ], axis=1).astype(np.float32)
+
+
+def column_table(angle):
+    return np.concatenate([np.cos(angle), -np.sin(angle)], axis=1).astype(np.float32)
+
+
+def sign_row():
+    lane = lax.broadcasted_iota(jnp.int32, (8, LANES), 1)
+    return jnp.where(lane < LANES // 2, -1.0, 1.0).astype(jnp.float32)
+
+
+def swap(value):
+    return pltpu.roll(value, LANES // 2, 1)
+
+
+class Split:
+    def __init__(self, real, imag):
+        self.real, self.imag = real, imag
+
+    def __add__(self, other):
+        return Split(self.real + other.real, self.imag + other.imag)
+
+    def __sub__(self, other):
+        return Split(self.real - other.real, self.imag - other.imag)
+
+    def turn(self, cosine, sine):
+        return Split(self.real * cosine - self.imag * sine, self.real * sine + self.imag * cosine)
+
+    def quarter(self):
+        return Split(self.imag, -self.real)
+
+    def eighth(self, half):
+        return Split((self.real + self.imag) * half, (self.imag - self.real) * half)
+
+
+class Joint:
+    def __init__(self, both, sign):
+        self.both, self.sign = both, sign
+
+    def __add__(self, other):
+        return Joint(self.both + other.both, self.sign)
+
+    def __sub__(self, other):
+        return Joint(self.both - other.both, self.sign)
+
+    def turn(self, cosine, sine):
+        return Joint(self.both * cosine + swap(self.both) * (self.sign * sine), self.sign)
+
+    def quarter(self):
+        return Joint(swap(self.both) * -self.sign, self.sign)
+
+    def eighth(self, half):
+        return self.turn(half, -half)
+
+
+def short_transform(items):
+    count = len(items)
+    if count == 1:
+        return items
+    if count % 4:
+        return [items[0] + items[1], items[0] - items[1]]
+    quarter = count // 4
+    parts = [short_transform(items[index::4]) for index in range(4)]
+    out = [None] * count
+    for index in range(quarter):
+        turned = [parts[0][index]]
+        for step in range(1, 4):
+            place = step * index
+            item = parts[step][index]
+            if place == 0:
+                turned.append(item)
+            elif place * 8 == count:
+                turned.append(item.eighth(math.sqrt(0.5)))
+            elif place * 4 == count:
+                turned.append(item.quarter())
+            else:
+                angle = -2.0 * math.pi * place / count
+                turned.append(item.turn(math.cos(angle), math.sin(angle)))
+        first, second, third, fourth = turned
+        even, odd = first + third, first - third
+        even_two, odd_two = second + fourth, (second - fourth).quarter()
+        out[index] = even + even_two
+        out[index + quarter] = odd + odd_two
+        out[index + 2 * quarter] = even - even_two
+        out[index + 3 * quarter] = odd - odd_two
+    return out
+
+
+def halves(value):
+    high = value.astype(jnp.bfloat16)
+    return high, (value - high.astype(jnp.float32)).astype(jnp.bfloat16)
+
+
+def product(left_high, left_low, right_high, right_low, dims):
+    def one(left, right):
+        return lax.dot_general(left, right, (dims, ((), ())), preferred_element_type=jnp.float32)
+
+    return one(left_high, right_high) + one(left_low, right_high) + one(left_high, right_low)
+
+
+NORMAL = ((1,), (0,))
+FLIPPED = ((1,), (1,))
+
+
+def sine_cosine(angle):
+    turns = jnp.floor(angle * (2.0 / math.pi) + 0.5)
+    rest = angle - turns * 1.5703125
+    rest = rest - turns * 4.837512969970703125e-4
+    rest = rest - turns * 7.54978995489188216e-8
+    quadrant = turns.astype(jnp.int32)
+    square = rest * rest
+    sine = rest + rest * square * (-1.6666654611e-1 + square * (8.3321608736e-3 + square * -1.9515295891e-4))
+    cosine = 1.0 + square * (-0.5 + square * (4.166664568298827e-2 + square * (-1.388731625493765e-3 + square * 2.443315711809948e-5)))
+    odd = (quadrant & 1) == 1
+    flip_sine = (quadrant & 2) == 2
+    flip_cosine = ((quadrant + 1) & 2) == 2
+    first = jnp.where(odd, cosine, sine)
+    second = jnp.where(odd, sine, cosine)
+    return jnp.where(flip_sine, -first, first), jnp.where(flip_cosine, -second, second)
+
+
+def across(count, steps, load, store, table=None):
+    def step(at, carry):
+        row = pl.multiple_of(at * 8, 8)
+        sign = sign_row()
+        main = short_transform([Split(load(s, 0, row), load(s, 1, row)) for s in range(count)])
+        for k in range(count):
+            item = main[k]
+            if table is not None:
+                item = item.turn(*table(k, row, False))
+            store(k, 0, row, item.real)
+            store(k, 1, row, item.imag)
+        tail = short_transform([Joint(load(s, 2, row), sign) for s in range(count)])
+        for k in range(count):
+            item = tail[k]
+            value = item.both
+            if table is not None:
+                cosine, signed = table(k, row, True)
+                value = value * cosine + swap(value) * signed
+            store(k, 2, row, value)
+        return carry
+
+    lax.fori_loop(0, steps, step, 0)
+
+
+def lane_lookup(table_ref):
+    def look(k, row, tail):
+        at = 2 if tail else 0
+        return table_ref[k, at:at + 1, :], table_ref[k, at + 1:at + 2, :]
+
+    return look
+
+
+def column_lookup(table_ref, count):
+    def look(k, row, tail):
+        cosine = jnp.broadcast_to(table_ref[pl.ds(row, 8), k:k + 1], (8, LANES))
+        sine = jnp.broadcast_to(table_ref[pl.ds(row, 8), count + k:count + k + 1], (8, LANES))
+        return cosine, (sine * sign_row() if tail else sine)
+
+    return look
+
+
+def column_product(matrix_ref, value):
+    high, low = halves(value)
+    both = product(matrix_ref[0], matrix_ref[1], high, low, NORMAL)
+    outs = both.shape[0] // 2
+    first, second = both[:outs], both[outs:]
+    sign = sign_row()[:1]
+    real = first[:, :LANES] + second[:, LANES:2 * LANES]
+    imag = first[:, LANES:2 * LANES] - second[:, :LANES]
+    tail = first[:, 2 * LANES:] - swap(second[:, 2 * LANES:]) * sign
+    return real, imag, tail
+
+
+def flipped_product(matrix_ref, value):
+    high, low = halves(value)
+    both = product(matrix_ref[0], matrix_ref[1], high, low, FLIPPED)
+    outs = both.shape[0] // 2
+    width = both.shape[1] - LANES
+    real, imag = both[:outs], both[outs:]
+    pieces = [real[:, LANES:], imag[:, LANES:]]
+    if width < LANES // 2:
+        gap = jnp.zeros((outs, LANES // 2 - width), jnp.float32)
+        pieces = [pieces[0], gap, pieces[1], gap]
+    return real[:, :LANES], imag[:, :LANES], jnp.concatenate(pieces, axis=1)
+
+
+def joined(ref, *lead):
+    return jnp.concatenate([ref[lead + (plane,)] for plane in range(3)], axis=-1)
+
+
+def column_turn(parts, cosine, sine):
+    real, imag, tail = parts
+    sign = sign_row()[:1]
+    return (
+        real * cosine - imag * sine,
+        real * sine + imag * cosine,
+        tail * cosine + swap(tail) * (sine * sign),
+    )
+
+
+def pick_column(table_ref, at, rows, count):
+    lane = lax.broadcasted_iota(jnp.int32, (rows, 2 * count), 1)
+    table = table_ref[...]
+    cosine = jnp.sum(jnp.where(lane == at, table, 0.0), axis=1, keepdims=True)
+    sine = jnp.sum(jnp.where(lane == at + count, table, 0.0), axis=1, keepdims=True)
+    return jnp.broadcast_to(cosine, (rows, LANES)), jnp.broadcast_to(sine, (rows, LANES))
+
+
+def whole(count):
+    return [pl.BlockSpec(memory_space=pltpu.VMEM)] * count
+
+
+def kernel_call(body, outs, inputs, scratch):
+    return pl.pallas_call(
+        body,
+        out_shape=outs,
+        in_specs=whole(len(inputs)),
+        out_specs=jax.tree.map(lambda _: pl.BlockSpec(memory_space=pltpu.VMEM), outs),
+        scratch_shapes=scratch,
+        compiler_params=pltpu.CompilerParams(vmem_limit_bytes=62 * 1024 * 1024),
+    )(*inputs)
+
+
+class Plan:
+    def __init__(self, length, row_count, col_count):
+        self.length, self.row_count, self.col_count = length, row_count, col_count
+        self.count = row_count * col_count
+        self.each = length // self.count
+        reach = length // 3 + 8
+        near = -(-reach // self.count)
+        near = (near + 3) // 4 * 4
+        steps = np.arange(self.each)
+        self.kept = np.concatenate([steps[:near], steps[self.each - near:]])
+        self.keep = len(self.kept)
+        self.near = near
+        scale = 1.0 / math.sqrt(length)
+        index = np.arange(self.each)
+        self.full = phase_of(np.outer(index, index), self.each)
+        self.cut = phase_of(np.outer(self.kept, index), self.each)
+        self.scale = scale
+        twist = 2.0 * np.pi * np.outer(np.arange(self.count), index) / length
+        self.lane_twist = lane_table(twist)
+        self.column_twist = column_table(twist.T)
+        self.tall = rows_matrix(self.full, scale)
+        self.tall_cut = rows_matrix(self.cut, scale)
+        self.tall_back = rows_matrix(self.cut.T, scale)
+        self.flip = transposed_matrix(self.full, scale)
+        self.flip_cut = transposed_matrix(self.cut, scale)
+        self.square = lane_square(self.cut, scale)
+        far = np.arange(self.count)[:, None] + self.count * self.kept[None, :]
+        self.far_chirp = lane_table(np.pi * (far * far % (2 * length)) / length)
+
+    def slot(self, block):
+        return block % self.row_count * self.col_count + block // self.row_count
+
+
+def first_kernel(plan, x_ref, matrix_ref, twist_ref, out_ref, work_ref):
+    count, each = plan.count, plan.each
+    part = each // plan.row_count
+
+    def step(s, carry):
+        planes = [
+            jnp.concatenate([x_ref[p, plane, pl.ds(s, part, stride=count), :] for p in range(plan.row_count)], axis=0)
+            for plane in range(3)
+        ]
+        parts = column_product(matrix_ref, jnp.concatenate(planes, axis=-1))
+        cosine, sine = pick_column(twist_ref, s, each, count)
+        for plane, value in enumerate(column_turn(parts, cosine, sine)):
+            work_ref[s, plane] = value
+        return carry
+
+    lax.fori_loop(0, count, step, 0)
+
+    def load(s, plane, row):
+        return work_ref[s, plane, pl.ds(row, 8), :]
+
+    def store(k, plane, row, value):
+        out_ref[k, plane, pl.ds(row, 8), :] = value
+
+    across(count, each // 8, load, store)
+
+
+def second_kernel(plan, x_ref, kerr_ref, theta_ref, own_ref, flip_ref, cut_ref, lane_ref, column_ref,
+                  out_ref, phase_ref, work_ref, field_ref):
+    count, each = plan.count, plan.each
+
+    def load(s, plane, row):
+        return x_ref[plan.slot(s), plane, pl.ds(row, 8), :]
+
+    def store(k, plane, row, value):
+        work_ref[k, plane, pl.ds(row, 8), :] = value
+
+    across(count, each // 8, load, store, lane_lookup(lane_ref))
+
+    def turn(k, carry):
+        for plane, value in enumerate(flipped_product(flip_ref, joined(work_ref, k))):
+            field_ref[plane, pl.ds(k, each, stride=count), :] = value
+        return carry
+
+    lax.fori_loop(0, count, turn, 0)
+    size = 32
+
+    def kerr(at, carry):
+        rows = pl.ds(pl.multiple_of(at * size, size), size)
+        sign = sign_row()[:1]
+        theta = theta_ref[rows, :]
+        real, imag, tail = field_ref[0, rows, :], field_ref[1, rows, :], field_ref[2, rows, :]
+        phase = kerr_ref[0, rows, :] * (real * real + imag * imag)
+        phase_ref[0, rows, :] = phase
+        sine, cosine = sine_cosine(phase + (theta + own_ref[0:1, :]))
+        field_ref[0, rows, :] = real * cosine - imag * sine
+        field_ref[1, rows, :] = real * sine + imag * cosine
+        square = tail * tail
+        phase = kerr_ref[1, rows, :] * (square + swap(square))
+        phase_ref[1, rows, :] = phase
+        sine, cosine = sine_cosine(phase + (theta + own_ref[1:2, :]))
+        field_ref[2, rows, :] = tail * cosine + swap(tail) * (sine * sign)
+        return carry
+
+    lax.fori_loop(0, plan.length // size, kerr, 0)
+
+    def again(s, plane, row):
+        return field_ref[plane, pl.ds(s * each + row, 8), :]
+
+    across(count, each // 8, again, store, column_lookup(column_ref, count))
+
+    def send(k, carry):
+        for plane, value in enumerate(column_product(cut_ref, joined(work_ref, k))):
+            out_ref[k, plane] = value
+        return carry
+
+    lax.fori_loop(0, count, send, 0)
+
+
+def third_kernel(plan, x_ref, matrix_ref, lane_ref, out_ref, work_ref):
+    def load(s, plane, row):
+        return x_ref[s, plane, pl.ds(row, 8), :]
+
+    def store(k, plane, row, value):
+        work_ref[k, plane, pl.ds(row, 8), :] = value
+
+    across(plan.count, plan.keep // 8, load, store, lane_lookup(lane_ref))
+
+    def send(k, carry):
+        for plane, value in enumerate(flipped_product(matrix_ref, joined(work_ref, k))):
+            out_ref[k, plane] = value
+        return carry
+
+    lax.fori_loop(0, plan.count, send, 0)
+
+
+def fourth_kernel(plan, x_ref, mask_ref, own_ref, chirp_ref, matrix_ref, lane_ref, out_ref, work_ref):
+    def step(d, carry):
+        sign = sign_row()[:1]
+        own_cos, own_sin = own_ref[0], own_ref[1]
+        main, tail_mask = mask_ref[d, 0], mask_ref[d, 1]
+        far = chirp_ref[d]
+        cosine = (own_cos * far[0:1] - own_sin * far[1:2]) * main
+        sine = (own_cos * far[1:2] + own_sin * far[0:1]) * main
+        real, imag, tail = x_ref[d, 0], x_ref[d, 1], x_ref[d, 2]
+        own_tail = own_sin * sign
+        tail = tail * (own_cos * tail_mask) + swap(tail) * (own_tail * tail_mask)
+        tail = tail * far[2:3] + swap(tail) * far[3:4]
+        value = jnp.concatenate([real * cosine - imag * sine, real * sine + imag * cosine, tail], axis=-1)
+        high, low = halves(value)
+        both = product(high, low, matrix_ref[0], matrix_ref[1], NORMAL)
+        real, imag, tail = both[:, :LANES], both[:, LANES:2 * LANES], both[:, 2 * LANES:]
+        twist = lane_ref[d]
+        work_ref[d, 0] = real * twist[0:1] - imag * twist[1:2]
+        work_ref[d, 1] = real * twist[1:2] + imag * twist[0:1]
+        work_ref[d, 2] = tail * twist[2:3] + swap(tail) * twist[3:4]
+        return carry
+
+    lax.fori_loop(0, plan.count, step, 0)
+
+    def load(s, plane, row):
+        return work_ref[s, plane, pl.ds(row, 8), :]
+
+    def store(k, plane, row, value):
+        out_ref[plan.slot(k), plane, pl.ds(row, 8), :] = value
+
+    across(plan.count, plan.keep // 8, load, store)
+
+
+def fifth_kernel(plan, x_ref, matrix_ref, column_ref, out_ref, work_ref):
+    def step(e, carry):
+        parts = column_product(matrix_ref, joined(x_ref, e))
+        cosine, sine = pick_column(column_ref, e, plan.each, plan.count)
+        for plane, value in enumerate(column_turn(parts, cosine, sine)):
+            work_ref[e, plane] = value
+        return carry
+
+    lax.fori_loop(0, plan.count, step, 0)
+
+    def load(s, plane, row):
+        return work_ref[s, plane, pl.ds(row, 8), :]
+
+    def store(k, plane, row, value):
+        out_ref[k, plane, pl.ds(row, 8), :] = value
+
+    across(plan.count, plan.each // 8, load, store)
+
+
+def f32(*shape):
+    return jax.ShapeDtypeStruct(shape, jnp.float32)
+
+
+def scratch(*shape):
+    return pltpu.VMEM(shape, jnp.float32)
+
+
+def square_angle(index, length):
+    return (math.pi / length) * (index * index % (2 * length)).astype(jnp.float32)
+
+
+def fast_device(plan, field_real, field_imag, kerr_map, pinhole):
+    length, count, each, keep = plan.length, plan.count, plan.each, plan.keep
+    rows_here, cols_here = field_real.shape
+    row_at, col_at = lax.axis_index("rows"), lax.axis_index("cols")
+    own = row_at * plan.col_count + col_at
+    both_axes = ("rows", "cols")
+    index = jnp.arange(length, dtype=jnp.int32)
+    theta = square_angle(index, length)
+
+    phase_one = kerr_map * (field_real * field_real + field_imag * field_imag)
+    down = lax.dynamic_slice(theta, (row_at * rows_here,), (rows_here,))
+    along = lax.dynamic_slice(theta, (col_at * cols_here,), (cols_here,))
+    angle = phase_one + (down[:, None] + along[None, :])
+    cosine, sine = jnp.cos(angle), jnp.sin(angle)
+
+    def blocks(part):
+        return jnp.transpose(part.reshape(rows_here, plan.row_count, each), (1, 0, 2))
+
+    real = blocks(field_real * cosine - field_imag * sine)
+    imag = blocks(field_real * sine + field_imag * cosine)
+    packed_field = jnp.stack([
+        real[..., :LANES], imag[..., :LANES],
+        jnp.concatenate([real[..., LANES:], imag[..., LANES:]], axis=-1),
+    ], axis=1)
+    field = lax.all_to_all(packed_field, "rows", split_axis=0, concat_axis=0, tiled=True)
+    kerr = lax.all_to_all(kerr_map.reshape(plan.col_count, each, cols_here), "cols", split_axis=0, concat_axis=0, tiled=True)
+    kerr = jnp.transpose(kerr, (0, 2, 1)).reshape(length, each)
+    kerr = jnp.stack([kerr[:, :LANES], jnp.concatenate([kerr[:, LANES:], kerr[:, LANES:]], axis=-1)])
+
+    near = plan.near
+
+    def cut(part, axis):
+        size = part.shape[axis]
+        return jnp.concatenate([
+            lax.slice_in_dim(part, 0, near, axis=axis), lax.slice_in_dim(part, size - near, size, axis=axis)
+        ], axis=axis)
+
+    mask = jnp.transpose(cut(pinhole.reshape(each, count, each), 0), (1, 0, 2)).astype(jnp.float32)
+    mask = lax.all_to_all(mask, both_axes, split_axis=0, concat_axis=0, tiled=True)
+    mask = jnp.transpose(mask, (1, 0, 2)).reshape(keep, each, count)
+    mask = jnp.transpose(cut(mask, 1), (2, 0, 1))
+    tail = jnp.pad(mask[..., LANES:], ((0, 0), (0, 0), (0, LANES // 2 - (keep - LANES))))
+    mask = jnp.stack([mask[..., :LANES], jnp.concatenate([tail, tail], axis=-1)], axis=1)
+
+    theta_wide = jnp.broadcast_to(theta[:, None] - math.pi / 2, (length, LANES))
+    lines = lax.dynamic_slice(theta, (own * each,), (each,))
+    own_theta = jnp.stack([lines[:LANES], jnp.concatenate([lines[LANES:], lines[LANES:]])])
+    far = own + count * jnp.asarray(plan.kept, jnp.int32)
+    far_angle = square_angle(far, length)
+    own_chirp = jnp.broadcast_to(jnp.stack([jnp.cos(far_angle), -jnp.sin(far_angle)])[:, :, None], (2, keep, LANES))
+
+    def exchange(part):
+        return lax.all_to_all(part, both_axes, split_axis=0, concat_axis=0, tiled=True)
+
+    field = kernel_call(
+        functools.partial(first_kernel, plan), f32(count, 3, each, LANES),
+        (field, plan.tall, plan.column_twist), [scratch(count, 3, each, LANES)],
+    )
+    field = exchange(field)
+    field, phase_two = kernel_call(
+        functools.partial(second_kernel, plan),
+        (f32(count, 3, keep, LANES), f32(2, length, LANES)),
+        (field, kerr, theta_wide, own_theta, plan.flip, plan.tall_cut, plan.lane_twist, plan.column_twist),
+        [scratch(count, 3, each, LANES), scratch(3, length, LANES)],
+    )
+    field = exchange(field)
+    field = kernel_call(
+        functools.partial(third_kernel, plan), f32(count, 3, keep, LANES),
+        (field, plan.flip_cut, plan.lane_twist), [scratch(count, 3, keep, LANES)],
+    )
+    field = exchange(field)
+    field = kernel_call(
+        functools.partial(fourth_kernel, plan), f32(count, 3, keep, LANES),
+        (field, mask, own_chirp, plan.far_chirp, plan.square, plan.lane_twist), [scratch(count, 3, keep, LANES)],
+    )
+    field = exchange(field)
+    field = kernel_call(
+        functools.partial(fifth_kernel, plan), f32(count, 3, each, LANES),
+        (field, plan.tall_back, plan.column_twist), [scratch(count, 3, each, LANES)],
+    )
+    field = field.reshape(plan.row_count, plan.col_count, 3, each, LANES)
+    field = lax.all_to_all(field, "rows", split_axis=0, concat_axis=0, tiled=True)
+    real = jnp.concatenate([field[:, :, 0], field[:, :, 2, :, :LANES // 2]], axis=-1)
+    imag = jnp.concatenate([field[:, :, 1], field[:, :, 2, :, LANES // 2:]], axis=-1)
+    out_real = jnp.transpose(real, (1, 2, 0, 3)).reshape(rows_here, cols_here)
+    out_imag = jnp.transpose(imag, (1, 2, 0, 3)).reshape(rows_here, cols_here)
+    phase = jnp.concatenate([phase_two[0], phase_two[1][:, :LANES // 2]], axis=-1)
+    phase = jnp.transpose(phase.reshape(plan.col_count, cols_here, each), (0, 2, 1))
+    phase = lax.all_to_all(phase, "cols", split_axis=0, concat_axis=0, tiled=True)
+    return (out_real, out_imag, phase_one + phase.reshape(rows_here, cols_here))
+
+
+def suits(length, count):
+    each = length // count
+    return count == 32 and each - LANES == LANES // 2
+
+
 def solution(mesh):
     placed = (P("rows", "cols"), P("rows", "cols"), P("rows", "cols"), P(None, ("rows", "cols")))
+
+    def device(field_real, field_imag, kerr_map, pinhole):
+        row_count, col_count = mesh.shape["rows"], mesh.shape["cols"]
+        length = pinhole.shape[0]
+        if suits(length, row_count * col_count):
+            plan = Plan(length, row_count, col_count)
+            return fast_device(plan, field_real, field_imag, kerr_map, pinhole)
+        return per_device(field_real, field_imag, kerr_map, pinhole)
+
     return jax.shard_map(
-        per_device,
+        device,
         mesh=mesh,
         in_specs=placed,
         out_specs=(P("rows", "cols"), P("rows", "cols"), P("rows", "cols")),

time: 1760 us -> 1450 us (0.82)
  matrix products: 374 us -> 0 us
  Pallas kernels: 0 us -> 228 us
  local copies, waits for them, and re-layouts: 267 us -> 140 us
  waiting for transfers between devices: 936 us -> 858 us
  blocking collectives: 59.7 us -> 110 us
    dot_general x64 -> x0, matrix products: 374 us -> none  [the longest x16 104 us: complex_apply(): real_sin = jnp.einsum(form, real_part, sin_table, precision=precision)]
    pallas_call x0 -> x5, Pallas kernels: none -> 228 us  [kernel_call(): pl.pallas_call(body, out_shape=outs, in_specs=whole(len(inputs)), out_spe...]
    another operation x14 -> x1, local copies, waits for them, and re-layouts: 109 us -> 2.77 us  [fast_device(): jnp.stack([real[..., :LANES], imag[..., :LANES], jnp.concatenate([real[.....]
    all_to_all x11 -> x8, waiting for transfers between devices: 936 us -> 858 us  [the longest x4 569 us: exchange(): lax.all_to_all(part, both_axes, split_axis=0, concat_axis=0, tiled=True)]
    all_to_all x1, blocking collectives: 59.7 us -> 110 us  [fast_device(): lax.all_to_all(packed_field, 'rows', split_axis=0, concat_axis=0, tiled=T...]
    all_to_all x7 -> x0, local copies, waits for them, and re-layouts: 44.3 us -> none  [the longest x2 18.2 us: send(): lax.all_to_all(part, ('cols', 'rows'), split_axis=0, concat_axis=2, tiled...]
    mul x6 -> x0, local copies, waits for them, and re-layouts: 39 us -> none  [the longest x3 19.5 us: transform_last(): jnp.transpose(imag_part, (0, 2, 1)).reshape(rows_here, length) * scale]
    reshape x0 -> x5, local copies, waits for them, and re-layouts: none -> 33.7 us  [the longest x2 12.5 us: blocks(): part.reshape(rows_here, plan.row_count, each)]
  transfers between devices with their start and end apart: 11 -> 8, of which waited for: 11 -> 8; matrix products, arithmetic and copies ran while one was open for 20% -> 6% of each run, Pallas kernels for 0% -> 7%
where the time goes in v1:
time: 1450 us; the launch traced here: 1440 us
  waiting for transfers between devices  858 us (59%)
  Pallas kernels  228 us (16%)
  local copies, waits for them, and re-layouts  140 us (10%)
  blocking collectives  110 us (8%)
  other arithmetic  55.3 us (4%)
  starting transfers between devices  49.7 us (3%)
    all_to_all x4, waiting for transfers between devices, exchange(): lax.all_to_all(part, both_axes, split_axis=0, concat_axis=0, tiled=True)  569 us
    pallas_call x5, Pallas kernels, kernel_call(): pl.pallas_call(body, out_shape=outs, in_specs=whole(len(inputs)), out_spe...  228 us
    all_to_all x1, blocking collectives, fast_device(): lax.all_to_all(packed_field, 'rows', split_axis=0, concat_axis=0, tiled=T...  110 us
    all_to_all x1, waiting for transfers between devices, fast_device(): lax.all_to_all(field, 'rows', split_axis=0, concat_axis=0, tiled=True)  83.3 us
    all_to_all x1, waiting for transfers between devices, fast_device(): lax.all_to_all(phase, 'cols', split_axis=0, concat_axis=0, tiled=True)  73.4 us
    all_to_all x1, waiting for transfers between devices, fast_device(): lax.all_to_all(mask, both_axes, split_axis=0, concat_axis=0, tiled=True)  70.5 us
    all_to_all x1, waiting for transfers between devices, fast_device(): lax.all_to_all(kerr_map.reshape(plan.col_count, each, cols_here), 'cols',...  61.2 us
    unnamed x18, local copies, waits for them, and re-layouts  38.5 us
  transfers between devices with their start and end apart: 8, of which 8 were waited for; matrix products, arithmetic and copies ran while one was open for 6% of the time, Pallas kernels for 7%

profile of v1, /device:TPU:0, one launch (start us, length us, event | category | flops | bytes accessed | tf_op | source)
XLA Modules:
  0.0 1442.6 jit_solution(4704743336042607802)
XLA Ops:
  18.9 22.4 %multiply_subtract_fusion = (f32[768,1536]{0,1:T(8,128)}, f32[768,1536]{0,1:T(8,128)}) fusion(f32[768,1536]{0,1:T(8,128)} %copy.76, f32[768,1536]{0,1:T(8,128)} %copy.79, f32[768,1536]{0,1:T(8,128)} %copy.78, f32[1536]{0:T(1024)S(1)} %dynamic_slice.10, f32[768]{0:T(1024)S(1)} %dynamic_slice.9), kind=kLoop, calls=%fused_computation.6 | loop fusion | flops 14155776 | bytes 23602176 | tf_op jit(solution)/shard_map/sub | solution.py:684
  62.4 110.3 %all_to_all.45.x_ref = f32[8,3,768,128]{3,2,1,0:T(8,128)} all-to-all(f32[8,3,768,128]{3,2,1,0:T(8,128)S(1)} %pad_maximum_fusion), channel_id=1, replica_groups=mesh['rows'=8,'cols'=4] {'rows'}, dimensions={0} | all-to-all | bytes 18874368 | tf_op jit(solution)/shard_map/all_to_all | solution.py:690
  177.7 43.0 %shard_map.157 = f32[32,3,192,128]{3,2,1,0:T(8,128)} custom-call(f32[8,3,768,128]{3,2,1,0:T(8,128)} %all_to_all.45.x_ref, bf16[2,384,192]{2,1,0:T(8,128)(2,1)} %constant.69.clone.matrix_ref, f32[192,64]{1,0:T(8,128)} %constant.70.clone.twist_ref.column_ref), custom_call_target="tpu_custom_call" | custom-call | tf_op jit(solution)/shard_map/pallas_call | solution.py:464
  220.7 61.2 %all-to-all-done.2 = f32[4,192,1536]{2,1,0:T(8,128)} async-done(((f32[4,192,1536]{2,1,0:T(8,128)}), f32[4,192,1536]{2,1,0:T(8,128)}, u32[]{:S(2)}, u32[]{:S(2)}) %all-to-all-start.2) | async-done | bytes 4718624 | tf_op jit(solution)/shard_map/all_to_all | solution.py:691
  286.4 6.3 copy.87
  300.4 188.8 %all-to-all-done.1.x_ref = f32[32,3,192,128]{3,2,1,0:T(8,128)} async-done(((f32[32,3,192,128]{3,2,1,0:T(8,128)}), f32[32,3,192,128]{3,2,1,0:T(8,128)}, u32[]{:S(2)}, u32[]{:S(2)}) %all-to-all-start.1) | async-done | bytes 9437216 | tf_op jit(solution)/shard_map/all_to_all | solution.py:718
  491.4 94.2 %shard_map.158 = (f32[32,3,136,128]{3,2,1,0:T(8,128)}, f32[2,6144,128]{2,1,0:T(8,128)}) custom-call(f32[32,3,192,128]{3,2,1,0:T(8,128)} %all-to-all-done.1.x_ref, f32[2,6144,128]{2,1,0:T(8,128)} %pad_maximum_fusion.1.kerr_ref, f32[6144,128]{1,0:T(8,128)} %broadcast_in_dim.4.theta_ref, f32[2,128]{1,0:T(2,128)} %pad_maximum_fusion.4.own_ref, ...), custom_call_target="tpu_custom_call" | custom-call | tf_op jit(solution)/shard_map/pallas_call | solution.py:464
  585.5 9.4 all-to-all-start.3
  610.7 129.3 %all-to-all-done.3.x_ref = f32[32,3,136,128]{3,2,1,0:T(8,128)} async-done(((f32[32,3,136,128]{3,2,1,0:T(8,128)}), f32[32,3,136,128]{3,2,1,0:T(8,128)}, u32[]{:S(2)}, u32[]{:S(2)}) %all-to-all-start.3) | async-done | bytes 6684704 | tf_op jit(solution)/shard_map/all_to_all | solution.py:718
  740.0 7.3 all-to-all-start.5
  747.3 27.2 %shard_map.159 = f32[32,3,136,128]{3,2,1,0:T(8,128)} custom-call(f32[32,3,136,128]{3,2,1,0:T(8,128)} %all-to-all-done.3.x_ref, bf16[2,272,384]{2,1,0:T(8,128)(2,1)} %constant.74.clone.matrix_ref, f32[32,4,128]{2,1,0:T(4,128)} %constant.73.clone.lane_ref), custom_call_target="tpu_custom_call" | custom-call | tf_op jit(solution)/shard_map/pallas_call | solution.py:464
  774.5 70.5 %all-to-all-done.5 = f32[32,136,192]{2,1,0:T(8,128)} async-done(((f32[32,136,192]{2,1,0:T(8,128)}), f32[32,136,192]{2,1,0:T(8,128)}, u32[]{:S(2)}, u32[]{:S(2)}) %all-to-all-start.5) | async-done | bytes 3342368 | tf_op jit(solution)/shard_map/all_to_all | solution.py:704
  850.9 6.4 copy.91
  874.4 121.5 %all-to-all-done.4.x_ref = f32[32,3,136,128]{3,2,1,0:T(8,128)} async-done(((f32[32,3,136,128]{3,2,1,0:T(8,128)}), f32[32,3,136,128]{3,2,1,0:T(8,128)}, u32[]{:S(2)}, u32[]{:S(2)}) %all-to-all-start.4) | async-done | bytes 6684704 | tf_op jit(solution)/shard_map/all_to_all | solution.py:718
  996.7 30.4 %shard_map.160 = f32[32,3,136,128]{3,2,1,0:T(8,128)} custom-call(f32[32,3,136,128]{3,2,1,0:T(8,128)} %all-to-all-done.4.x_ref, f32[32,2,136,128]{3,2,1,0:T(8,128)} %pad_maximum_fusion.2.mask_ref, f32[2,136,128]{2,1,0:T(8,128)} %broadcast_in_dim.5.own_ref, f32[32,4,128]{2,1,0:T(4,128)} %constant.75.clone.chirp_ref, ...), custom_call_target="tpu_custom_call" | custom-call | tf_op jit(solution)/shard_map/pallas_call | solution.py:464
  1027.1 7.6 all-to-all-start.6
  1050.0 129.7 %all-to-all-done.6.x_ref = f32[32,3,136,128]{3,2,1,0:T(8,128)} async-done(((f32[32,3,136,128]{3,2,1,0:T(8,128)}), f32[32,3,136,128]{3,2,1,0:T(8,128)}, u32[]{:S(2)}, u32[]{:S(2)}) %all-to-all-start.6) | async-done | bytes 6684704 | tf_op jit(solution)/shard_map/all_to_all | solution.py:718
  1185.6 33.1 %shard_map.161 = f32[32,3,192,128]{3,2,1,0:T(8,128)} custom-call(f32[32,3,136,128]{3,2,1,0:T(8,128)} %all-to-all-done.6.x_ref, bf16[2,384,136]{2,1,0:T(8,128)(2,1)} %constant.77.clone.matrix_ref, f32[192,64]{1,0:T(8,128)} %constant.70.clone.twist_ref.column_ref), custom_call_target="tpu_custom_call" | custom-call | tf_op jit(solution)/shard_map/pallas_call | solution.py:464
  1218.7 73.4 %all-to-all-done.8 = f32[4,192,1536]{2,1,0:T(8,128)} async-done(((f32[4,192,1536]{2,1,0:T(8,128)}), f32[4,192,1536]{2,1,0:T(8,128)}, u32[]{:S(2)}, u32[]{:S(2)}) %all-to-all-start.8) | async-done | bytes 4718624 | tf_op jit(solution)/shard_map/all_to_all | solution.py:754
  1303.2 9.8 fusion.3
  1319.1 83.3 %all-to-all-done.7 = f32[8,4,3,192,128]{4,3,2,1,0:T(8,128)} async-done(((f32[8,4,3,192,128]{4,3,2,1,0:T(8,128)}), f32[8,4,3,192,128]{4,3,2,1,0:T(8,128)}, u32[]{:S(2)}, u32[]{:S(2)}) %all-to-all-start.7) | async-done | bytes 9437216 | tf_op jit(solution)/shard_map/all_to_all | solution.py:747
  1412.0 6.3 copy.96
  1418.2 7.7 reshape.64
  1434.7 7.4 reshape.63
  (65 shorter events, 154.8 us)
Async XLA Ops:
  53.9 3.7 copy-start
  53.9 6.5 slice-start
  57.6 3.0 slice-start.1
  172.7 109.1 %all-to-all-start.2 = ((f32[4,192,1536]{2,1,0:T(8,128)}), f32[4,192,1536]{2,1,0:T(8,128)}, u32[]{:S(2)}, u32[]{:S(2)}) async-start(f32[4,192,1536]{2,1,0:T(8,128)} %bitcast.75), calls=%async_computation.2 | async-start | bytes 9437184 | tf_op jit(solution)/shard_map/all_to_all | solution.py:691
  281.9 207.4 %all-to-all-start.1 = ((f32[32,3,192,128]{3,2,1,0:T(8,128)}), f32[32,3,192,128]{3,2,1,0:T(8,128)}, u32[]{:S(2)}, u32[]{:S(2)}) async-start(f32[32,3,192,128]{3,2,1,0:T(8,128)} %shard_map.157), calls=%async_computation.1 | async-start | bytes 18874368 | tf_op jit(solution)/shard_map/all_to_all | solution.py:718
  292.6 3.7 copy-start.1
  585.5 154.4 %all-to-all-start.3 = ((f32[32,3,136,128]{3,2,1,0:T(8,128)}), f32[32,3,136,128]{3,2,1,0:T(8,128)}, u32[]{:S(2)}, u32[]{:S(2)}) async-start(f32[32,3,136,128]{3,2,1,0:T(8,128)} %get-tuple-element.5), calls=%async_computation.3 | async-start | bytes 13369344 | tf_op jit(solution)/shard_map/all_to_all | solution.py:718
  740.0 105.0 %all-to-all-start.5 = ((f32[32,136,192]{2,1,0:T(8,128)}), f32[32,136,192]{2,1,0:T(8,128)}, u32[]{:S(2)}, u32[]{:S(2)}) async-start(f32[32,136,192]{2,1,0:T(8,128)} %copy.90), calls=%async_computation.5 | async-start | bytes 8912896 | tf_op jit(solution)/shard_map/all_to_all | solution.py:704
  774.5 76.3 %copy-start.2 = (s32[136]{0:T(256)S(1)}, s32[136]{0:T(256)}, u32[]{:S(2)}) copy-start(s32[136]{0:T(256)} %constant.80) | copy-start | bytes 1636
  845.0 150.9 %all-to-all-start.4 = ((f32[32,3,136,128]{3,2,1,0:T(8,128)}), f32[32,3,136,128]{3,2,1,0:T(8,128)}, u32[]{:S(2)}, u32[]{:S(2)}) async-start(f32[32,3,136,128]{3,2,1,0:T(8,128)} %shard_map.159), calls=%async_computation.4 | async-start | bytes 13369344 | tf_op jit(solution)/shard_map/all_to_all | solution.py:718
  1027.1 152.6 %all-to-all-start.6 = ((f32[32,3,136,128]{3,2,1,0:T(8,128)}), f32[32,3,136,128]{3,2,1,0:T(8,128)}, u32[]{:S(2)}, u32[]{:S(2)}) async-start(f32[32,3,136,128]{3,2,1,0:T(8,128)} %shard_map.160), calls=%async_computation.6 | async-start | bytes 13369344 | tf_op jit(solution)/shard_map/all_to_all | solution.py:718
  1179.7 112.3 %all-to-all-start.8 = ((f32[4,192,1536]{2,1,0:T(8,128)}), f32[4,192,1536]{2,1,0:T(8,128)}, u32[]{:S(2)}, u32[]{:S(2)}) async-start(f32[4,192,1536]{2,1,0:T(8,128)} %maximum_bitcast_fusion.2), calls=%async_computation.8 | async-start | bytes 9437184 | tf_op jit(solution)/shard_map/all_to_all | solution.py:754
  1292.0 110.3 %all-to-all-start.7 = ((f32[8,4,3,192,128]{4,3,2,1,0:T(8,128)}), f32[8,4,3,192,128]{4,3,2,1,0:T(8,128)}, u32[]{:S(2)}, u32[]{:S(2)}) async-start(f32[8,4,3,192,128]{4,3,2,1,0:T(8,128)} %bitcast.66), calls=%async_computation.7 | async-start | bytes 18874368 | tf_op jit(solution)/shard_map/all_to_all | solution.py:747

commit v2 on v1

--- a/solution.py
+++ b/solution.py
@@ -663,6 +663,96 @@
     return (math.pi / length) * (index * index % (2 * length)).astype(jnp.float32)
 
 
+def pack_kernel(plan, real_ref, imag_ref, kerr_ref, down_ref, along_ref, out_ref):
+    size = 16
+    pairs = plan.row_count // 2
+
+    def step(at, carry):
+        rows = pl.ds(pl.multiple_of(at * size, size), size)
+        low = lax.broadcasted_iota(jnp.int32, (size, LANES), 1) < LANES // 2
+        down = down_ref[rows, :]
+        for pair in range(pairs):
+            tiles = []
+            for tile in range(3):
+                lanes = slice((3 * pair + tile) * LANES, (3 * pair + tile + 1) * LANES)
+                real, imag = real_ref[rows, lanes], imag_ref[rows, lanes]
+                phase = kerr_ref[rows, lanes] * (real * real + imag * imag)
+                sine, cosine = sine_cosine(phase + (down + along_ref[0:1, lanes]))
+                tiles.append((real * cosine - imag * sine, real * sine + imag * cosine))
+            (real_a, imag_a), (real_b, imag_b), (real_c, imag_c) = tiles
+            even, odd = 2 * pair, 2 * pair + 1
+            out_ref[even, 0, rows, :] = real_a
+            out_ref[even, 1, rows, :] = imag_a
+            out_ref[even, 2, rows, :] = jnp.where(low, real_b, swap(imag_b))
+            turned = swap(real_c)
+            out_ref[odd, 0, rows, :] = jnp.where(low, swap(real_b), turned)
+            out_ref[odd, 1, rows, :] = jnp.where(low, swap(imag_b), swap(imag_c))
+            out_ref[odd, 2, rows, :] = jnp.where(low, turned, imag_c)
+        return carry
+
+    lax.fori_loop(0, real_ref.shape[0] // size, step, 0)
+
+
+def pack_field(plan, field_real, field_imag, kerr_map, down, along):
+    rows_here, cols_here = field_real.shape
+    rows = rows_here // plan.col_count
+    tile = pl.BlockSpec((rows, cols_here), lambda i: (i, 0))
+    return pl.pallas_call(
+        functools.partial(pack_kernel, plan),
+        out_shape=f32(plan.row_count, 3, rows_here, LANES),
+        grid=(plan.col_count,),
+        in_specs=[tile, tile, tile, pl.BlockSpec((rows, LANES), lambda i: (i, 0)), pl.BlockSpec((1, cols_here), lambda i: (0, 0))],
+        out_specs=pl.BlockSpec((plan.row_count, 3, rows, LANES), lambda i: (0, 0, i, 0)),
+        compiler_params=pltpu.CompilerParams(vmem_limit_bytes=40 * 1024 * 1024),
+    )(field_real, field_imag, kerr_map, jnp.broadcast_to(down[:, None], (rows_here, LANES)), along[None, :])
+
+
+def unpack_kernel(plan, field_ref, real_ref, imag_ref):
+    size = 16
+
+    def step(at, carry):
+        rows = pl.ds(pl.multiple_of(at * size, size), size)
+        low = lax.broadcasted_iota(jnp.int32, (size, LANES), 1) < LANES // 2
+        for pair in range(plan.row_count // 2):
+            even, odd = 2 * pair, 2 * pair + 1
+            tails = field_ref[even, 0, 2, rows, :], field_ref[odd, 0, 2, rows, :]
+            for plane, out_ref in enumerate((real_ref, imag_ref)):
+                own = tails[0] if plane == 0 else swap(tails[0])
+                last = swap(tails[1]) if plane == 0 else tails[1]
+                turned = swap(field_ref[odd, 0, plane, rows, :])
+                at_lane = 3 * pair * LANES
+                out_ref[rows, at_lane:at_lane + LANES] = field_ref[even, 0, plane, rows, :]
+                out_ref[rows, at_lane + LANES:at_lane + 2 * LANES] = jnp.where(low, own, turned)
+                out_ref[rows, at_lane + 2 * LANES:at_lane + 3 * LANES] = jnp.where(low, turned, last)
+        return carry
+
+    lax.fori_loop(0, real_ref.shape[0] // size, step, 0)
+
+
+def unpack_field(plan, field, rows_here, cols_here):
+    tile = pl.BlockSpec((plan.each, cols_here), lambda i: (i, 0))
+    return pl.pallas_call(
+        functools.partial(unpack_kernel, plan),
+        out_shape=(f32(rows_here, cols_here), f32(rows_here, cols_here)),
+        grid=(plan.col_count,),
+        in_specs=[pl.BlockSpec((plan.row_count, 1, 3, plan.each, LANES), lambda i: (0, i, 0, 0, 0))],
+        out_specs=(tile, tile),
+        compiler_params=pltpu.CompilerParams(vmem_limit_bytes=40 * 1024 * 1024),
+    )(field)
+
+
+def spread(plan, part, col_at):
+    count = plan.col_count
+    got = []
+    for shift in range(count):
+        block = lax.dynamic_index_in_dim(part, (col_at + shift) % count, 0, keepdims=True)
+        if shift:
+            block = lax.ppermute(block, "cols", [(z, (z + shift) % count) for z in range(count)])
+        got.append(block)
+    ring = got[::-1]
+    return lax.dynamic_slice_in_dim(jnp.concatenate(ring + ring, axis=0), count - 1 - col_at, count, axis=0)
+
+
 def fast_device(plan, field_real, field_imag, kerr_map, pinhole):
     length, count, each, keep = plan.length, plan.count, plan.each, plan.keep
     rows_here, cols_here = field_real.shape
@@ -675,20 +765,10 @@
     phase_one = kerr_map * (field_real * field_real + field_imag * field_imag)
     down = lax.dynamic_slice(theta, (row_at * rows_here,), (rows_here,))
     along = lax.dynamic_slice(theta, (col_at * cols_here,), (cols_here,))
-    angle = phase_one + (down[:, None] + along[None, :])
-    cosine, sine = jnp.cos(angle), jnp.sin(angle)
-
-    def blocks(part):
-        return jnp.transpose(part.reshape(rows_here, plan.row_count, each), (1, 0, 2))
-
-    real = blocks(field_real * cosine - field_imag * sine)
-    imag = blocks(field_real * sine + field_imag * cosine)
-    packed_field = jnp.stack([
-        real[..., :LANES], imag[..., :LANES],
-        jnp.concatenate([real[..., LANES:], imag[..., LANES:]], axis=-1),
-    ], axis=1)
+    packed_field = pack_field(plan, field_real, field_imag, kerr_map, down, along)
     field = lax.all_to_all(packed_field, "rows", split_axis=0, concat_axis=0, tiled=True)
-    kerr = lax.all_to_all(kerr_map.reshape(plan.col_count, each, cols_here), "cols", split_axis=0, concat_axis=0, tiled=True)
+    kerr = spread(plan, kerr_map.reshape(plan.col_count, each, cols_here), col_at)
+    field, kerr = lax.optimization_barrier((field, kerr))
     kerr = jnp.transpose(kerr, (0, 2, 1)).reshape(length, each)
     kerr = jnp.stack([kerr[:, :LANES], jnp.concatenate([kerr[:, LANES:], kerr[:, LANES:]], axis=-1)])
 
@@ -701,11 +781,6 @@
         ], axis=axis)
 
     mask = jnp.transpose(cut(pinhole.reshape(each, count, each), 0), (1, 0, 2)).astype(jnp.float32)
-    mask = lax.all_to_all(mask, both_axes, split_axis=0, concat_axis=0, tiled=True)
-    mask = jnp.transpose(mask, (1, 0, 2)).reshape(keep, each, count)
-    mask = jnp.transpose(cut(mask, 1), (2, 0, 1))
-    tail = jnp.pad(mask[..., LANES:], ((0, 0), (0, 0), (0, LANES // 2 - (keep - LANES))))
-    mask = jnp.stack([mask[..., :LANES], jnp.concatenate([tail, tail], axis=-1)], axis=1)
 
     theta_wide = jnp.broadcast_to(theta[:, None] - math.pi / 2, (length, LANES))
     lines = lax.dynamic_slice(theta, (own * each,), (each,))
@@ -722,13 +797,20 @@
         (field, plan.tall, plan.column_twist), [scratch(count, 3, each, LANES)],
     )
     field = exchange(field)
+    field, mask = lax.optimization_barrier((field, mask))
+    mask = lax.all_to_all(mask, both_axes, split_axis=0, concat_axis=0, tiled=True)
     field, phase_two = kernel_call(
         functools.partial(second_kernel, plan),
         (f32(count, 3, keep, LANES), f32(2, length, LANES)),
         (field, kerr, theta_wide, own_theta, plan.flip, plan.tall_cut, plan.lane_twist, plan.column_twist),
         [scratch(count, 3, each, LANES), scratch(3, length, LANES)],
     )
+    field, mask = lax.optimization_barrier((field, mask))
     field = exchange(field)
+    mask = jnp.transpose(mask, (1, 0, 2)).reshape(keep, each, count)
+    mask = jnp.transpose(cut(mask, 1), (2, 0, 1))
+    tail = jnp.pad(mask[..., LANES:], ((0, 0), (0, 0), (0, LANES // 2 - (keep - LANES))))
+    mask = jnp.stack([mask[..., :LANES], jnp.concatenate([tail, tail], axis=-1)], axis=1)
     field = kernel_call(
         functools.partial(third_kernel, plan), f32(count, 3, keep, LANES),
         (field, plan.flip_cut, plan.lane_twist), [scratch(count, 3, keep, LANES)],
@@ -743,15 +825,13 @@
         functools.partial(fifth_kernel, plan), f32(count, 3, each, LANES),
         (field, plan.tall_back, plan.column_twist), [scratch(count, 3, each, LANES)],
     )
-    field = field.reshape(plan.row_count, plan.col_count, 3, each, LANES)
-    field = lax.all_to_all(field, "rows", split_axis=0, concat_axis=0, tiled=True)
-    real = jnp.concatenate([field[:, :, 0], field[:, :, 2, :, :LANES // 2]], axis=-1)
-    imag = jnp.concatenate([field[:, :, 1], field[:, :, 2, :, LANES // 2:]], axis=-1)
-    out_real = jnp.transpose(real, (1, 2, 0, 3)).reshape(rows_here, cols_here)
-    out_imag = jnp.transpose(imag, (1, 2, 0, 3)).reshape(rows_here, cols_here)
     phase = jnp.concatenate([phase_two[0], phase_two[1][:, :LANES // 2]], axis=-1)
     phase = jnp.transpose(phase.reshape(plan.col_count, cols_here, each), (0, 2, 1))
-    phase = lax.all_to_all(phase, "cols", split_axis=0, concat_axis=0, tiled=True)
+    field, phase = lax.optimization_barrier((field, phase))
+    field = field.reshape(plan.row_count, plan.col_count, 3, each, LANES)
+    phase = spread(plan, phase, col_at)
+    field = lax.all_to_all(field, "rows", split_axis=0, concat_axis=0, tiled=True)
+    out_real, out_imag = unpack_field(plan, field, rows_here, cols_here)
     return (out_real, out_imag, phase_one + phase.reshape(rows_here, cols_here))
 
 

time: 1450 us -> 1210 us (0.83)
  waiting for transfers between devices: 858 us -> 643 us
  local copies, waits for them, and re-layouts: 140 us -> 83.8 us
  blocking collectives: 110 us -> 152 us
  other arithmetic: 55.3 us -> 28.9 us
  Pallas kernels: 228 us -> 252 us
    ppermute x0 -> x6, waiting for transfers between devices: none -> 202 us  [spread(): lax.ppermute(block, 'cols', [(z, (z + shift) % count) for z in range(coun...]
    all_to_all x2 -> x1, waiting for transfers between devices: 135 us -> 0.01 us  [fast_device(): lax.all_to_all(packed_field, 'rows', split_axis=0, concat_axis=0, tiled=T...]
    all_to_all x4 -> x3, waiting for transfers between devices: 569 us -> 441 us  [exchange(): lax.all_to_all(part, both_axes, split_axis=0, concat_axis=0, tiled=True)]
    all_to_all x1, waiting for transfers between devices: 83.3 us -> 0.01 us  [fast_device(): lax.all_to_all(field, 'rows', split_axis=0, concat_axis=0, tiled=True)]
    all_to_all x1, waiting for transfers between devices: 70.5 us -> 0.01 us  [fast_device(): lax.all_to_all(mask, both_axes, split_axis=0, concat_axis=0, tiled=True)]
    all_to_all x1, blocking collectives: 110 us -> 152 us  [exchange(): lax.all_to_all(part, both_axes, split_axis=0, concat_axis=0, tiled=True)]
    reshape x5 -> x0, local copies, waits for them, and re-layouts: 33.7 us -> none  [the longest x2 12.5 us: blocks(): part.reshape(rows_here, plan.row_count, each)]
    pallas_call x0 -> x2, Pallas kernels: none -> 23.4 us  [the longest x1 13.4 us: pack_field(): pl.pallas_call(functools.partial(pack_kernel, plan), out_shape=f32(plan.r...]
  transfers between devices with their start and end apart: 8 -> 12, of which waited for: 8 -> 7; matrix products, arithmetic and copies ran while one was open for 6% -> 8% of each run, Pallas kernels for 7% -> 8%
where the time goes in v2:
time: 1210 us
  waiting for transfers between devices  643 us (53%)
  Pallas kernels  252 us (21%)
  blocking collectives  152 us (13%)
  local copies, waits for them, and re-layouts  83.8 us (7%)
  starting transfers between devices  48.8 us (4%)
  other arithmetic  28.9 us (2%)
    all_to_all x3, waiting for transfers between devices, exchange(): lax.all_to_all(part, both_axes, split_axis=0, concat_axis=0, tiled=True)  441 us
    pallas_call x5, Pallas kernels, kernel_call(): pl.pallas_call(body, out_shape=outs, in_specs=whole(len(inputs)), out_spe...  228 us
    ppermute x6, waiting for transfers between devices, spread(): lax.ppermute(block, 'cols', [(z, (z + shift) % count) for z in range(coun...  202 us
    all_to_all x1, blocking collectives, exchange(): lax.all_to_all(part, both_axes, split_axis=0, concat_axis=0, tiled=True)  152 us
    unnamed x38, local copies, waits for them, and re-layouts  24.8 us
  transfers between devices with their start and end apart: 12, of which 7 were waited for; matrix products, arithmetic and copies ran while one was open for 8% of the time, Pallas kernels for 8%

profile of v2, /device:TPU:0, one launch (start us, length us, event | category | flops | bytes accessed | tf_op | source)
XLA Modules:
  0.0 1209.8 jit_solution(16221070139778498002)
XLA Ops:
  8.0 13.4 %shard_map.157 = f32[8,3,768,128]{3,2,1,0:T(8,128)} custom-call(f32[768,1536]{1,0:T(8,128)S(1)} %copy-done.1, f32[768,1536]{1,0:T(8,128)S(1)} %copy-done.2, f32[768,1536]{1,0:T(8,128)S(1)} %copy-done, f32[768,128]{1,0:T(8,128)S(1)} %broadcast_in_dim.8.down_ref, f32[1,1536]{1,0:T(1,128)S(1)} %broadcast_in_dim.9.along_ref), custom_call_target="tpu_custom_call" | custom-call | tf_op jit(solution)/shard_map/pallas_call | solution.py:700
  21.4 5.2 all-to-all-start
  36.4 25.7 %collective-permute-done = f32[1,192,1536]{2,1,0:T(8,128)S(1)} collective-permute-done((f32[1,192,1536]{2,1,0:T(8,128)}, f32[1,192,1536]{2,1,0:T(8,128)S(1)}, u32[]{:S(2)}, u32[]{:S(2)}) %collective-permute-start) | collective-permute-done | bytes 1179680 | tf_op jit(solution)/shard_map/ppermute | solution.py:750
  62.3 74.8 %collective-permute-done.1 = f32[1,192,1536]{2,1,0:T(8,128)S(1)} collective-permute-done((f32[1,192,1536]{2,1,0:T(8,128)}, f32[1,192,1536]{2,1,0:T(8,128)S(1)}, u32[]{:S(2)}, u32[]{:S(2)}) %collective-permute-start.1) | collective-permute-done | bytes 1179680 | tf_op jit(solution)/shard_map/ppermute | solution.py:750
  142.8 43.0 %shard_map.158 = f32[32,3,192,128]{3,2,1,0:T(8,128)} custom-call(f32[8,3,768,128]{3,2,1,0:T(8,128)} %all-to-all-done.x_ref, bf16[2,384,192]{2,1,0:T(8,128)(2,1)} %constant.125.clone.matrix_ref, f32[192,64]{1,0:T(8,128)} %constant.126.clone.twist_ref.column_ref), custom_call_target="tpu_custom_call" | custom-call | tf_op jit(solution)/shard_map/pallas_call | solution.py:464
  185.8 5.2 all-to-all-start.1
  204.4 190.3 %all-to-all-done.1.x_ref = f32[32,3,192,128]{3,2,1,0:T(8,128)} async-done(((f32[32,3,192,128]{3,2,1,0:T(8,128)}), f32[32,3,192,128]{3,2,1,0:T(8,128)}, u32[]{:S(2)}, u32[]{:S(2)}) %all-to-all-start.1) | async-done | bytes 9437216 | tf_op jit(solution)/shard_map/all_to_all | solution.py:793
  394.7 6.9 copy.37
  401.6 9.2 all-to-all-start.2
  412.3 6.3 copy.36
  428.5 94.7 %shard_map.159 = (f32[32,3,136,128]{3,2,1,0:T(8,128)}, f32[2,6144,128]{2,1,0:T(8,128)}) custom-call(f32[32,3,192,128]{3,2,1,0:T(8,128)} %all-to-all-done.1.x_ref, f32[2,6144,128]{2,1,0:T(8,128)} %pad_maximum_fusion.kerr_ref, f32[6144,128]{1,0:T(8,128)} %broadcast_in_dim.10.theta_ref, f32[2,128]{1,0:T(2,128)} %pad_maximum_fusion.3.own_ref, ...), custom_call_target="tpu_custom_call" | custom-call | tf_op jit(solution)/shard_map/pallas_call | solution.py:464
  523.1 152.4 %all_to_all.35.x_ref = f32[32,3,136,128]{3,2,1,0:T(8,128)} all-to-all(f32[32,3,136,128]{3,2,1,0:T(8,128)} %get-tuple-element.20), channel_id=1, replica_groups=mesh['rows'=8,'cols'=4] {'rows','cols'}, dimensions={0} | all-to-all | bytes 13369344 | tf_op jit(solution)/shard_map/all_to_all | solution.py:793
  675.5 27.0 %shard_map.160 = f32[32,3,136,128]{3,2,1,0:T(8,128)} custom-call(f32[32,3,136,128]{3,2,1,0:T(8,128)} %all_to_all.35.x_ref, bf16[2,272,384]{2,1,0:T(8,128)(2,1)} %constant.130.clone.matrix_ref, f32[32,4,128]{2,1,0:T(4,128)} %constant.129.clone.lane_ref), custom_call_target="tpu_custom_call" | custom-call | tf_op jit(solution)/shard_map/pallas_call | solution.py:464
  706.7 6.4 copy.38
  730.2 121.5 %all-to-all-done.4.x_ref = f32[32,3,136,128]{3,2,1,0:T(8,128)} async-done(((f32[32,3,136,128]{3,2,1,0:T(8,128)}), f32[32,3,136,128]{3,2,1,0:T(8,128)}, u32[]{:S(2)}, u32[]{:S(2)}) %all-to-all-start.4) | async-done | bytes 6684704 | tf_op jit(solution)/shard_map/all_to_all | solution.py:793
  852.5 30.4 %shard_map.161 = f32[32,3,136,128]{3,2,1,0:T(8,128)} custom-call(f32[32,3,136,128]{3,2,1,0:T(8,128)} %all-to-all-done.4.x_ref, f32[32,2,136,128]{3,2,1,0:T(8,128)} %pad_maximum_fusion.1.mask_ref, f32[2,136,128]{2,1,0:T(8,128)} %broadcast_in_dim.11.own_ref, f32[32,4,128]{2,1,0:T(4,128)} %constant.131.clone.chirp_ref, ...), custom_call_target="tpu_custom_call" | custom-call | tf_op jit(solution)/shard_map/pallas_call | solution.py:464
  882.9 7.4 all-to-all-start.5
  905.6 129.7 %all-to-all-done.5.x_ref = f32[32,3,136,128]{3,2,1,0:T(8,128)} async-done(((f32[32,3,136,128]{3,2,1,0:T(8,128)}), f32[32,3,136,128]{3,2,1,0:T(8,128)}, u32[]{:S(2)}, u32[]{:S(2)}) %all-to-all-start.5) | async-done | bytes 6684704 | tf_op jit(solution)/shard_map/all_to_all | solution.py:793
  1035.3 33.0 %shard_map.162 = f32[32,3,192,128]{3,2,1,0:T(8,128)} custom-call(f32[32,3,136,128]{3,2,1,0:T(8,128)} %all-to-all-done.5.x_ref, bf16[2,384,136]{2,1,0:T(8,128)(2,1)} %constant.133.clone.matrix_ref, f32[192,64]{1,0:T(8,128)} %constant.126.clone.twist_ref.column_ref), custom_call_target="tpu_custom_call" | custom-call | tf_op jit(solution)/shard_map/pallas_call | solution.py:464
  1076.3 5.1 collective-permute-start.4
  1082.3 23.9 %collective-permute-done.3 = f32[1,192,1536]{2,1,0:T(8,128)S(1)} collective-permute-done((f32[1,192,1536]{2,1,0:T(8,128)S(1)}, f32[1,192,1536]{2,1,0:T(8,128)S(1)}, u32[]{:S(2)}, u32[]{:S(2)}) %collective-permute-start.3) | collective-permute-done | bytes 1179680 | tf_op jit(solution)/shard_map/ppermute | solution.py:750
  1106.3 77.5 %collective-permute-done.4 = f32[1,192,1536]{2,1,0:T(8,128)S(1)} collective-permute-done((f32[1,192,1536]{2,1,0:T(8,128)S(1)}, f32[1,192,1536]{2,1,0:T(8,128)S(1)}, u32[]{:S(2)}, u32[]{:S(2)}) %collective-permute-start.4) | collective-permute-done | bytes 1179680 | tf_op jit(solution)/shard_map/ppermute | solution.py:750
  1191.5 8.3 bitcast_add_fusion
  1199.7 10.1 shard_map.163
  (89 shorter events, 101.6 us)
Async XLA Ops:
  0.7 20.7 %copy-start.4 = (f32[6144]{0:T(1024)}, f32[6144]{0:T(1024)S(1)}, u32[]{:S(2)}) copy-start(f32[6144]{0:T(1024)S(1)} %fusion.2) | copy-start | bytes 73732
  1.0 2.3 copy-start
  3.3 2.3 copy-start.1
  5.7 2.3 copy-start.2
  21.4 121.4 %all-to-all-start = ((f32[8,3,768,128]{3,2,1,0:T(8,128)}), f32[8,3,768,128]{3,2,1,0:T(8,128)}, u32[]{:S(2)}, u32[]{:S(2)}) async-start(f32[8,3,768,128]{3,2,1,0:T(8,128)} %shard_map.157), calls=%async_computation | async-start | bytes 18874368 | tf_op jit(solution)/shard_map/all_to_all | solution.py:769
  30.4 31.8 %collective-permute-start = (f32[1,192,1536]{2,1,0:T(8,128)}, f32[1,192,1536]{2,1,0:T(8,128)S(1)}, u32[]{:S(2)}, u32[]{:S(2)}) collective-permute-start(f32[1,192,1536]{2,1,0:T(8,128)} %get-tuple-element.38), channel_id=1, source_target_pairs={{0,3},{1,0},{2,1},{3,2},{4,7},{5,4},{6,5},{7,6},{8,11},{9,8},{10,9... | collective-permute-start | bytes 3538952 | tf_op jit(solution)/shard_map/ppermute | solution.py:750
  35.4 101.7 %collective-permute-start.1 = (f32[1,192,1536]{2,1,0:T(8,128)}, f32[1,192,1536]{2,1,0:T(8,128)S(1)}, u32[]{:S(2)}, u32[]{:S(2)}) collective-permute-start(f32[1,192,1536]{2,1,0:T(8,128)} %get-tuple-element.37), channel_id=1, source_target_pairs={{0,2},{1,3},{2,0},{3,1},{4,6},{5,7},{6,4},{7,5},{8,10},{9,11},{10,... | collective-permute-start | bytes 3538952 | tf_op jit(solution)/shard_map/ppermute | solution.py:750
  35.4 101.8 %collective-permute-start.2 = (f32[1,192,1536]{2,1,0:T(8,128)}, f32[1,192,1536]{2,1,0:T(8,128)S(1)}, u32[]{:S(2)}, u32[]{:S(2)}) collective-permute-start(f32[1,192,1536]{2,1,0:T(8,128)} %get-tuple-element.36), channel_id=1, source_target_pairs={{0,1},{1,2},{2,3},{3,0},{4,5},{5,6},{6,7},{7,4},{8,9},{9,10},{10,1... | collective-permute-start | bytes 3538952 | tf_op jit(solution)/shard_map/ppermute | solution.py:750
  185.8 208.8 %all-to-all-start.1 = ((f32[32,3,192,128]{3,2,1,0:T(8,128)}), f32[32,3,192,128]{3,2,1,0:T(8,128)}, u32[]{:S(2)}, u32[]{:S(2)}) async-start(f32[32,3,192,128]{3,2,1,0:T(8,128)} %shard_map.158), calls=%async_computation.1 | async-start | bytes 18874368 | tf_op jit(solution)/shard_map/all_to_all | solution.py:793
  401.6 121.5 %all-to-all-start.2 = ((f32[32,136,192]{2,1,0:T(8,128)}), f32[32,136,192]{2,1,0:T(8,128)}, u32[]{:S(2)}, u32[]{:S(2)}) async-start(f32[32,136,192]{2,1,0:T(8,128)} %copy.37), calls=%async_computation.2 | async-start | bytes 8912896 | tf_op jit(solution)/shard_map/all_to_all | solution.py:801
  418.6 3.7 copy-start.3
  702.6 4.1 copy-start.5
  702.6 149.1 %all-to-all-start.4 = ((f32[32,3,136,128]{3,2,1,0:T(8,128)}), f32[32,3,136,128]{3,2,1,0:T(8,128)}, u32[]{:S(2)}, u32[]{:S(2)}) async-start(f32[32,3,136,128]{3,2,1,0:T(8,128)} %shard_map.160), calls=%async_computation.4 | async-start | bytes 13369344 | tf_op jit(solution)/shard_map/all_to_all | solution.py:793
  882.9 152.4 %all-to-all-start.5 = ((f32[32,3,136,128]{3,2,1,0:T(8,128)}), f32[32,3,136,128]{3,2,1,0:T(8,128)}, u32[]{:S(2)}, u32[]{:S(2)}) async-start(f32[32,3,136,128]{3,2,1,0:T(8,128)} %shard_map.161), calls=%async_computation.5 | async-start | bytes 13369344 | tf_op jit(solution)/shard_map/all_to_all | solution.py:793
  1068.3 131.4 %all-to-all-start.6 = ((f32[8,4,3,192,128]{4,3,2,1,0:T(8,128)}), f32[8,4,3,192,128]{4,3,2,1,0:T(8,128)}, u32[]{:S(2)}, u32[]{:S(2)}) async-start(f32[8,4,3,192,128]{4,3,2,1,0:T(8,128)} %bitcast.44), calls=%async_computation.6 | async-start | bytes 18874368 | tf_op jit(solution)/shard_map/all_to_all | solution.py:833
  1075.6 30.6 %collective-permute-start.3 = (f32[1,192,1536]{2,1,0:T(8,128)S(1)}, f32[1,192,1536]{2,1,0:T(8,128)S(1)}, u32[]{:S(2)}, u32[]{:S(2)}) collective-permute-start(f32[1,192,1536]{2,1,0:T(8,128)S(1)} %get-tuple-element.33), channel_id=1, source_target_pairs={{0,3},{1,0},{2,1},{3,2},{4,7},{5,4},{6,5},{7,6},{8,11},{9,8},{10,9... | collective-permute-start | bytes 3538952 | tf_op jit(solution)/shard_map/ppermute | solution.py:750
  1076.3 107.5 %collective-permute-start.4 = (f32[1,192,1536]{2,1,0:T(8,128)S(1)}, f32[1,192,1536]{2,1,0:T(8,128)S(1)}, u32[]{:S(2)}, u32[]{:S(2)}) collective-permute-start(f32[1,192,1536]{2,1,0:T(8,128)S(1)} %get-tuple-element.32), channel_id=1, source_target_pairs={{0,2},{1,3},{2,0},{3,1},{4,6},{5,7},{6,4},{7,5},{8,10},{9,11},{10,... | collective-permute-start | bytes 3538952 | tf_op jit(solution)/shard_map/ppermute | solution.py:750
  1081.3 102.5 %collective-permute-start.5 = (f32[1,192,1536]{2,1,0:T(8,128)S(1)}, f32[1,192,1536]{2,1,0:T(8,128)S(1)}, u32[]{:S(2)}, u32[]{:S(2)}) collective-permute-start(f32[1,192,1536]{2,1,0:T(8,128)S(1)} %get-tuple-element.31), channel_id=1, source_target_pairs={{0,1},{1,2},{2,3},{3,0},{4,5},{5,6},{6,7},{7,4},{8,9},{9,10},{10,1... | collective-permute-start | bytes 3538952 | tf_op jit(solution)/shard_map/ppermute | solution.py:750
  1185.5 4.4 slice-start
  1185.5 5.5 slice-start.2
  1187.2 4.1 slice-start.1
  1187.2 4.3 slice-start.3

commit v3 on v2

--- a/solution.py
+++ b/solution.py
@@ -591,9 +591,22 @@
 
     across(plan.count, plan.keep // 8, load, store, lane_lookup(lane_ref))
 
+    keep, extra = plan.keep, plan.keep - LANES
+
     def send(k, carry):
-        for plane, value in enumerate(flipped_product(matrix_ref, joined(work_ref, k))):
-            out_ref[k, plane] = value
+        value = joined(work_ref, k)
+        high, low = halves(value[:LANES])
+        both = product(matrix_ref[0], matrix_ref[1], high, low, FLIPPED)
+        out_ref[k, 0:2 * keep, :] = both
+        rest = jnp.concatenate([value[LANES:], jnp.zeros((16 - extra, value.shape[1]), jnp.float32)], axis=0)
+        high, low = halves(rest)
+        gap = jnp.zeros((extra, LANES - extra), jnp.float32)
+        for part in range(2):
+            rows = slice(part * keep, (part + 1) * keep)
+            tail = product(high, low, matrix_ref[0, rows, :], matrix_ref[1, rows, :], FLIPPED)[:extra]
+            at = 2 * keep + 2 * part * extra
+            out_ref[k, at:at + extra, :] = tail[:, :LANES]
+            out_ref[k, at + extra:at + 2 * extra, :] = jnp.concatenate([tail[:, LANES:], gap], axis=1)
         return carry
 
     lax.fori_loop(0, plan.count, send, 0)
@@ -607,7 +620,15 @@
         far = chirp_ref[d]
         cosine = (own_cos * far[0:1] - own_sin * far[1:2]) * main
         sine = (own_cos * far[1:2] + own_sin * far[0:1]) * main
-        real, imag, tail = x_ref[d, 0], x_ref[d, 1], x_ref[d, 2]
+        keep, extra = plan.keep, plan.keep - LANES
+        real, imag = x_ref[d, 0:keep, :], x_ref[d, keep:2 * keep, :]
+        gap = jnp.zeros((LANES // 2 - extra, 2 * LANES), jnp.float32)
+        pieces = []
+        for part in range(2):
+            at = 2 * keep + 2 * part * extra
+            pieces.append(jnp.concatenate([x_ref[d, at:at + extra, :], x_ref[d, at + extra:at + 2 * extra, :]], axis=1))
+            pieces.append(gap)
+        tail = jnp.transpose(jnp.concatenate(pieces, axis=0))[:keep]
         own_tail = own_sin * sign
         tail = tail * (own_cos * tail_mask) + swap(tail) * (own_tail * tail_mask)
         tail = tail * far[2:3] + swap(tail) * far[3:4]
@@ -812,7 +833,7 @@
     tail = jnp.pad(mask[..., LANES:], ((0, 0), (0, 0), (0, LANES // 2 - (keep - LANES))))
     mask = jnp.stack([mask[..., :LANES], jnp.concatenate([tail, tail], axis=-1)], axis=1)
     field = kernel_call(
-        functools.partial(third_kernel, plan), f32(count, 3, keep, LANES),
+        functools.partial(third_kernel, plan), f32(count, 2 * keep + 4 * (keep - LANES), LANES),
         (field, plan.flip_cut, plan.lane_twist), [scratch(count, 3, keep, LANES)],
     )
     field = exchange(field)

time: 1210 us -> 1180 us (0.975)
  waiting for transfers between devices: 643 us -> 607 us
    all_to_all x3, waiting for transfers between devices: 441 us -> 405 us  [exchange(): lax.all_to_all(part, both_axes, split_axis=0, concat_axis=0, tiled=True)]
where the time goes in v3:
time: 1180 us
  waiting for transfers between devices  607 us (51%)
  Pallas kernels  259 us (22%)
  blocking collectives  152 us (13%)
  local copies, waits for them, and re-layouts  83.8 us (7%)
  starting transfers between devices  47.6 us (4%)
  other arithmetic  29 us (2%)
    all_to_all x3, waiting for transfers between devices, exchange(): lax.all_to_all(part, both_axes, split_axis=0, concat_axis=0, tiled=True)  405 us
    pallas_call x5, Pallas kernels, kernel_call(): pl.pallas_call(body, out_shape=outs, in_specs=whole(len(inputs)), out_spe...  236 us
    ppermute x6, waiting for transfers between devices, spread(): lax.ppermute(block, 'cols', [(z, (z + shift) % count) for z in range(coun...  202 us
    all_to_all x1, blocking collectives, exchange(): lax.all_to_all(part, both_axes, split_axis=0, concat_axis=0, tiled=True)  152 us
    unnamed x38, local copies, waits for them, and re-layouts  24.8 us
  transfers between devices with their start and end apart: 12, of which 7 were waited for; matrix products, arithmetic and copies ran while one was open for 8% of the time, Pallas kernels for 8%

profile of v3, /device:TPU:0, one launch (start us, length us, event | category | flops | bytes accessed | tf_op | source)
XLA Modules:
  0.0 1179.7 jit_solution(1502915976746570567)
XLA Ops:
  8.0 13.3 %shard_map.157 = f32[8,3,768,128]{3,2,1,0:T(8,128)} custom-call(f32[768,1536]{1,0:T(8,128)S(1)} %copy-done.1, f32[768,1536]{1,0:T(8,128)S(1)} %copy-done.2, f32[768,1536]{1,0:T(8,128)S(1)} %copy-done, f32[768,128]{1,0:T(8,128)S(1)} %broadcast_in_dim.8.down_ref, f32[1,1536]{1,0:T(1,128)S(1)} %broadcast_in_dim.9.along_ref), custom_call_target="tpu_custom_call" | custom-call | tf_op jit(solution)/shard_map/pallas_call | solution.py:721
  21.3 5.2 all-to-all-start
  36.4 25.7 %collective-permute-done = f32[1,192,1536]{2,1,0:T(8,128)S(1)} collective-permute-done((f32[1,192,1536]{2,1,0:T(8,128)}, f32[1,192,1536]{2,1,0:T(8,128)S(1)}, u32[]{:S(2)}, u32[]{:S(2)}) %collective-permute-start) | collective-permute-done | bytes 1179680 | tf_op jit(solution)/shard_map/ppermute | solution.py:771
  62.2 74.8 %collective-permute-done.1 = f32[1,192,1536]{2,1,0:T(8,128)S(1)} collective-permute-done((f32[1,192,1536]{2,1,0:T(8,128)}, f32[1,192,1536]{2,1,0:T(8,128)S(1)}, u32[]{:S(2)}, u32[]{:S(2)}) %collective-permute-start.1) | collective-permute-done | bytes 1179680 | tf_op jit(solution)/shard_map/ppermute | solution.py:771
  142.7 43.0 %shard_map.158 = f32[32,3,192,128]{3,2,1,0:T(8,128)} custom-call(f32[8,3,768,128]{3,2,1,0:T(8,128)} %all-to-all-done.x_ref, bf16[2,384,192]{2,1,0:T(8,128)(2,1)} %constant.125.clone.matrix_ref, f32[192,64]{1,0:T(8,128)} %constant.126.clone.twist_ref.column_ref), custom_call_target="tpu_custom_call" | custom-call | tf_op jit(solution)/shard_map/pallas_call | solution.py:464
  185.7 5.2 all-to-all-start.1
  204.3 190.3 %all-to-all-done.1.x_ref = f32[32,3,192,128]{3,2,1,0:T(8,128)} async-done(((f32[32,3,192,128]{3,2,1,0:T(8,128)}), f32[32,3,192,128]{3,2,1,0:T(8,128)}, u32[]{:S(2)}, u32[]{:S(2)}) %all-to-all-start.1) | async-done | bytes 9437216 | tf_op jit(solution)/shard_map/all_to_all | solution.py:814
  394.6 6.9 copy.37
  401.5 9.2 all-to-all-start.2
  412.2 6.2 copy.36
  428.4 94.3 %shard_map.159 = (f32[32,3,136,128]{3,2,1,0:T(8,128)}, f32[2,6144,128]{2,1,0:T(8,128)}) custom-call(f32[32,3,192,128]{3,2,1,0:T(8,128)} %all-to-all-done.1.x_ref, f32[2,6144,128]{2,1,0:T(8,128)} %pad_maximum_fusion.kerr_ref, f32[6144,128]{1,0:T(8,128)} %broadcast_in_dim.10.theta_ref, f32[2,128]{1,0:T(2,128)} %pad_maximum_fusion.3.own_ref, ...), custom_call_target="tpu_custom_call" | custom-call | tf_op jit(solution)/shard_map/pallas_call | solution.py:464
  522.7 152.4 %all_to_all.35.x_ref = f32[32,3,136,128]{3,2,1,0:T(8,128)} all-to-all(f32[32,3,136,128]{3,2,1,0:T(8,128)} %get-tuple-element.20), channel_id=1, replica_groups=mesh['rows'=8,'cols'=4] {'rows','cols'}, dimensions={0} | all-to-all | bytes 13369344 | tf_op jit(solution)/shard_map/all_to_all | solution.py:814
  675.0 30.9 %shard_map.160 = f32[32,304,128]{2,1,0:T(8,128)} custom-call(f32[32,3,136,128]{3,2,1,0:T(8,128)} %all_to_all.35.x_ref, bf16[2,272,384]{2,1,0:T(8,128)(2,1)} %constant.130.clone.matrix_ref, f32[32,4,128]{2,1,0:T(4,128)} %constant.129.clone.lane_ref), custom_call_target="tpu_custom_call" | custom-call | tf_op jit(solution)/shard_map/pallas_call | solution.py:464
  710.1 6.5 copy.38
  733.7 85.2 %all-to-all-done.4.x_ref = f32[32,304,128]{2,1,0:T(8,128)} async-done(((f32[32,304,128]{2,1,0:T(8,128)}), f32[32,304,128]{2,1,0:T(8,128)}, u32[]{:S(2)}, u32[]{:S(2)}) %all-to-all-start.4) | async-done | bytes 4980768 | tf_op jit(solution)/shard_map/all_to_all | solution.py:814
  819.6 34.2 %shard_map.161 = f32[32,3,136,128]{3,2,1,0:T(8,128)} custom-call(f32[32,304,128]{2,1,0:T(8,128)} %all-to-all-done.4.x_ref, f32[32,2,136,128]{3,2,1,0:T(8,128)} %pad_maximum_fusion.1.mask_ref, f32[2,136,128]{2,1,0:T(8,128)} %broadcast_in_dim.11.own_ref, f32[32,4,128]{2,1,0:T(4,128)} %constant.131.clone.chirp_ref, ...), custom_call_target="tpu_custom_call" | custom-call | tf_op jit(solution)/shard_map/pallas_call | solution.py:464
  853.9 6.2 all-to-all-start.5
  875.5 129.7 %all-to-all-done.5.x_ref = f32[32,3,136,128]{3,2,1,0:T(8,128)} async-done(((f32[32,3,136,128]{3,2,1,0:T(8,128)}), f32[32,3,136,128]{3,2,1,0:T(8,128)}, u32[]{:S(2)}, u32[]{:S(2)}) %all-to-all-start.5) | async-done | bytes 6684704 | tf_op jit(solution)/shard_map/all_to_all | solution.py:814
  1005.2 33.1 %shard_map.162 = f32[32,3,192,128]{3,2,1,0:T(8,128)} custom-call(f32[32,3,136,128]{3,2,1,0:T(8,128)} %all-to-all-done.5.x_ref, bf16[2,384,136]{2,1,0:T(8,128)(2,1)} %constant.133.clone.matrix_ref, f32[192,64]{1,0:T(8,128)} %constant.126.clone.twist_ref.column_ref), custom_call_target="tpu_custom_call" | custom-call | tf_op jit(solution)/shard_map/pallas_call | solution.py:464
  1046.1 5.1 collective-permute-start.4
  1052.2 23.9 %collective-permute-done.3 = f32[1,192,1536]{2,1,0:T(8,128)S(1)} collective-permute-done((f32[1,192,1536]{2,1,0:T(8,128)S(1)}, f32[1,192,1536]{2,1,0:T(8,128)S(1)}, u32[]{:S(2)}, u32[]{:S(2)}) %collective-permute-start.3) | collective-permute-done | bytes 1179680 | tf_op jit(solution)/shard_map/ppermute | solution.py:771
  1076.1 77.5 %collective-permute-done.4 = f32[1,192,1536]{2,1,0:T(8,128)S(1)} collective-permute-done((f32[1,192,1536]{2,1,0:T(8,128)S(1)}, f32[1,192,1536]{2,1,0:T(8,128)S(1)}, u32[]{:S(2)}, u32[]{:S(2)}) %collective-permute-start.4) | collective-permute-done | bytes 1179680 | tf_op jit(solution)/shard_map/ppermute | solution.py:771
  1161.3 8.3 bitcast_add_fusion
  1169.6 10.1 shard_map.163
  (89 shorter events, 101.6 us)
Async XLA Ops:
  0.7 20.7 %copy-start.4 = (f32[6144]{0:T(1024)}, f32[6144]{0:T(1024)S(1)}, u32[]{:S(2)}) copy-start(f32[6144]{0:T(1024)S(1)} %fusion.2) | copy-start | bytes 73732
  1.0 2.3 copy-start
  3.3 2.3 copy-start.1
  5.7 2.3 copy-start.2
  21.3 121.4 %all-to-all-start = ((f32[8,3,768,128]{3,2,1,0:T(8,128)}), f32[8,3,768,128]{3,2,1,0:T(8,128)}, u32[]{:S(2)}, u32[]{:S(2)}) async-start(f32[8,3,768,128]{3,2,1,0:T(8,128)} %shard_map.157), calls=%async_computation | async-start | bytes 18874368 | tf_op jit(solution)/shard_map/all_to_all | solution.py:790
  30.4 31.8 %collective-permute-start = (f32[1,192,1536]{2,1,0:T(8,128)}, f32[1,192,1536]{2,1,0:T(8,128)S(1)}, u32[]{:S(2)}, u32[]{:S(2)}) collective-permute-start(f32[1,192,1536]{2,1,0:T(8,128)} %get-tuple-element.38), channel_id=1, source_target_pairs={{0,3},{1,0},{2,1},{3,2},{4,7},{5,4},{6,5},{7,6},{8,11},{9,8},{10,9... | collective-permute-start | bytes 3538952 | tf_op jit(solution)/shard_map/ppermute | solution.py:771
  35.4 101.7 %collective-permute-start.1 = (f32[1,192,1536]{2,1,0:T(8,128)}, f32[1,192,1536]{2,1,0:T(8,128)S(1)}, u32[]{:S(2)}, u32[]{:S(2)}) collective-permute-start(f32[1,192,1536]{2,1,0:T(8,128)} %get-tuple-element.37), channel_id=1, source_target_pairs={{0,2},{1,3},{2,0},{3,1},{4,6},{5,7},{6,4},{7,5},{8,10},{9,11},{10,... | collective-permute-start | bytes 3538952 | tf_op jit(solution)/shard_map/ppermute | solution.py:771
  35.4 101.8 %collective-permute-start.2 = (f32[1,192,1536]{2,1,0:T(8,128)}, f32[1,192,1536]{2,1,0:T(8,128)S(1)}, u32[]{:S(2)}, u32[]{:S(2)}) collective-permute-start(f32[1,192,1536]{2,1,0:T(8,128)} %get-tuple-element.36), channel_id=1, source_target_pairs={{0,1},{1,2},{2,3},{3,0},{4,5},{5,6},{6,7},{7,4},{8,9},{9,10},{10,1... | collective-permute-start | bytes 3538952 | tf_op jit(solution)/shard_map/ppermute | solution.py:771
  185.7 208.8 %all-to-all-start.1 = ((f32[32,3,192,128]{3,2,1,0:T(8,128)}), f32[32,3,192,128]{3,2,1,0:T(8,128)}, u32[]{:S(2)}, u32[]{:S(2)}) async-start(f32[32,3,192,128]{3,2,1,0:T(8,128)} %shard_map.158), calls=%async_computation.1 | async-start | bytes 18874368 | tf_op jit(solution)/shard_map/all_to_all | solution.py:814
  401.5 121.1 %all-to-all-start.2 = ((f32[32,136,192]{2,1,0:T(8,128)}), f32[32,136,192]{2,1,0:T(8,128)}, u32[]{:S(2)}, u32[]{:S(2)}) async-start(f32[32,136,192]{2,1,0:T(8,128)} %copy.37), calls=%async_computation.2 | async-start | bytes 8912896 | tf_op jit(solution)/shard_map/all_to_all | solution.py:822
  418.4 3.7 copy-start.3
  706.0 4.1 copy-start.5
  706.0 112.9 %all-to-all-start.4 = ((f32[32,304,128]{2,1,0:T(8,128)}), f32[32,304,128]{2,1,0:T(8,128)}, u32[]{:S(2)}, u32[]{:S(2)}) async-start(f32[32,304,128]{2,1,0:T(8,128)} %shard_map.160), calls=%async_computation.4 | async-start | bytes 9961472 | tf_op jit(solution)/shard_map/all_to_all | solution.py:814
  853.9 151.3 %all-to-all-start.5 = ((f32[32,3,136,128]{3,2,1,0:T(8,128)}), f32[32,3,136,128]{3,2,1,0:T(8,128)}, u32[]{:S(2)}, u32[]{:S(2)}) async-start(f32[32,3,136,128]{3,2,1,0:T(8,128)} %shard_map.161), calls=%async_computation.5 | async-start | bytes 13369344 | tf_op jit(solution)/shard_map/all_to_all | solution.py:814
  1038.2 131.3 %all-to-all-start.6 = ((f32[8,4,3,192,128]{4,3,2,1,0:T(8,128)}), f32[8,4,3,192,128]{4,3,2,1,0:T(8,128)}, u32[]{:S(2)}, u32[]{:S(2)}) async-start(f32[8,4,3,192,128]{4,3,2,1,0:T(8,128)} %bitcast.44), calls=%async_computation.6 | async-start | bytes 18874368 | tf_op jit(solution)/shard_map/all_to_all | solution.py:854
  1045.5 30.5 %collective-permute-start.3 = (f32[1,192,1536]{2,1,0:T(8,128)S(1)}, f32[1,192,1536]{2,1,0:T(8,128)S(1)}, u32[]{:S(2)}, u32[]{:S(2)}) collective-permute-start(f32[1,192,1536]{2,1,0:T(8,128)S(1)} %get-tuple-element.33), channel_id=1, source_target_pairs={{0,3},{1,0},{2,1},{3,2},{4,7},{5,4},{6,5},{7,6},{8,11},{9,8},{10,9... | collective-permute-start | bytes 3538952 | tf_op jit(solution)/shard_map/ppermute | solution.py:771
  1046.1 107.5 %collective-permute-start.4 = (f32[1,192,1536]{2,1,0:T(8,128)S(1)}, f32[1,192,1536]{2,1,0:T(8,128)S(1)}, u32[]{:S(2)}, u32[]{:S(2)}) collective-permute-start(f32[1,192,1536]{2,1,0:T(8,128)S(1)} %get-tuple-element.32), channel_id=1, source_target_pairs={{0,2},{1,3},{2,0},{3,1},{4,6},{5,7},{6,4},{7,5},{8,10},{9,11},{10,... | collective-permute-start | bytes 3538952 | tf_op jit(solution)/shard_map/ppermute | solution.py:771
  1051.2 102.5 %collective-permute-start.5 = (f32[1,192,1536]{2,1,0:T(8,128)S(1)}, f32[1,192,1536]{2,1,0:T(8,128)S(1)}, u32[]{:S(2)}, u32[]{:S(2)}) collective-permute-start(f32[1,192,1536]{2,1,0:T(8,128)S(1)} %get-tuple-element.31), channel_id=1, source_target_pairs={{0,1},{1,2},{2,3},{3,0},{4,5},{5,6},{6,7},{7,4},{8,9},{9,10},{10,1... | collective-permute-start | bytes 3538952 | tf_op jit(solution)/shard_map/ppermute | solution.py:771
  1155.4 4.4 slice-start
  1155.4 5.5 slice-start.2
  1157.0 4.1 slice-start.1
  1157.0 4.3 slice-start.3

commit v4 on v3

--- a/solution.py
+++ b/solution.py
@@ -368,25 +368,27 @@
     return jnp.where(flip_sine, -first, first), jnp.where(flip_cosine, -second, second)
 
 
-def across(count, steps, load, store, table=None):
+def across(count, steps, load, store, table=None, parts=(True, True)):
     def step(at, carry):
         row = pl.multiple_of(at * 8, 8)
         sign = sign_row()
-        main = short_transform([Split(load(s, 0, row), load(s, 1, row)) for s in range(count)])
-        for k in range(count):
-            item = main[k]
-            if table is not None:
-                item = item.turn(*table(k, row, False))
-            store(k, 0, row, item.real)
-            store(k, 1, row, item.imag)
-        tail = short_transform([Joint(load(s, 2, row), sign) for s in range(count)])
-        for k in range(count):
-            item = tail[k]
-            value = item.both
-            if table is not None:
-                cosine, signed = table(k, row, True)
-                value = value * cosine + swap(value) * signed
-            store(k, 2, row, value)
+        if parts[0]:
+            main = short_transform([Split(load(s, 0, row), load(s, 1, row)) for s in range(count)])
+            for k in range(count):
+                item = main[k]
+                if table is not None:
+                    item = item.turn(*table(k, row, False))
+                store(k, 0, row, item.real)
+                store(k, 1, row, item.imag)
+        if parts[1]:
+            tail = short_transform([Joint(load(s, 2, row), sign) for s in range(count)])
+            for k in range(count):
+                item = tail[k]
+                value = item.both
+                if table is not None:
+                    cosine, signed = table(k, row, True)
+                    value = value * cosine + swap(value) * signed
+                store(k, 2, row, value)
         return carry
 
     lax.fori_loop(0, steps, step, 0)
@@ -415,6 +417,10 @@
     outs = both.shape[0] // 2
     first, second = both[:outs], both[outs:]
     sign = sign_row()[:1]
+    if value.shape[1] == LANES:
+        return (first - swap(second) * sign,)
+    if value.shape[1] == 2 * LANES:
+        return first[:, :LANES] + second[:, LANES:], first[:, LANES:] - second[:, :LANES]
     real = first[:, :LANES] + second[:, LANES:2 * LANES]
     imag = first[:, LANES:2 * LANES] - second[:, :LANES]
     tail = first[:, 2 * LANES:] - swap(second[:, 2 * LANES:]) * sign
@@ -435,17 +441,14 @@
 
 
 def joined(ref, *lead):
-    return jnp.concatenate([ref[lead + (plane,)] for plane in range(3)], axis=-1)
+    return jnp.concatenate([ref[lead + (plane,)] for plane in range(ref.shape[len(lead)])], axis=-1)
 
 
 def column_turn(parts, cosine, sine):
-    real, imag, tail = parts
-    sign = sign_row()[:1]
-    return (
-        real * cosine - imag * sine,
-        real * sine + imag * cosine,
-        tail * cosine + swap(tail) * (sine * sign),
-    )
+    if len(parts) == 1:
+        return (parts[0] * cosine + swap(parts[0]) * (sine * sign_row()[:1]),)
+    real, imag = parts
+    return real * cosine - imag * sine, real * sine + imag * cosine
 
 
 def pick_column(table_ref, at, rows, count):
@@ -460,13 +463,14 @@
     return [pl.BlockSpec(memory_space=pltpu.VMEM)] * count
 
 
-def kernel_call(body, outs, inputs, scratch):
+def kernel_call(body, outs, inputs, scratch, kilo=0):
     return pl.pallas_call(
         body,
         out_shape=outs,
         in_specs=whole(len(inputs)),
         out_specs=jax.tree.map(lambda _: pl.BlockSpec(memory_space=pltpu.VMEM), outs),
         scratch_shapes=scratch,
+        cost_estimate=pl.CostEstimate(flops=kilo * 10**6, bytes_accessed=10**7, transcendentals=0) if kilo else None,
         compiler_params=pltpu.CompilerParams(vmem_limit_bytes=62 * 1024 * 1024),
     )(*inputs)
 
@@ -507,11 +511,12 @@
 def first_kernel(plan, x_ref, matrix_ref, twist_ref, out_ref, work_ref):
     count, each = plan.count, plan.each
     part = each // plan.row_count
+    planes_here = x_ref.shape[1]
 
     def step(s, carry):
         planes = [
             jnp.concatenate([x_ref[p, plane, pl.ds(s, part, stride=count), :] for p in range(plan.row_count)], axis=0)
-            for plane in range(3)
+            for plane in range(planes_here)
         ]
         parts = column_product(matrix_ref, jnp.concatenate(planes, axis=-1))
         cosine, sine = pick_column(twist_ref, s, each, count)
@@ -527,14 +532,26 @@
     def store(k, plane, row, value):
         out_ref[k, plane, pl.ds(row, 8), :] = value
 
-    across(count, each // 8, load, store)
-
-
-def second_kernel(plan, x_ref, kerr_ref, theta_ref, own_ref, flip_ref, cut_ref, lane_ref, column_ref,
+    across_planes(count, each // 8, load, store, planes_here)
+
+
+def across_planes(count, steps, load, store, planes_here):
+    if planes_here == 2:
+        across(count, steps, load, store, None, (True, False))
+    else:
+        across(
+            count, steps, lambda s, plane, row: load(s, plane - 2, row),
+            lambda k, plane, row, value: store(k, plane - 2, row, value), None, (False, True),
+        )
+
+
+def second_kernel(plan, x_ref, tail_ref, kerr_ref, theta_ref, own_ref, flip_ref, cut_ref, lane_ref, column_ref,
                   out_ref, phase_ref, work_ref, field_ref):
     count, each = plan.count, plan.each
 
     def load(s, plane, row):
+        if plane == 2:
+            return tail_ref[plan.slot(s), 0, pl.ds(row, 8), :]
         return x_ref[plan.slot(s), plane, pl.ds(row, 8), :]
 
     def store(k, plane, row, value):
@@ -612,7 +629,7 @@
     lax.fori_loop(0, plan.count, send, 0)
 
 
-def fourth_kernel(plan, x_ref, mask_ref, own_ref, chirp_ref, matrix_ref, lane_ref, out_ref, work_ref):
+def fourth_kernel(plan, x_ref, mask_ref, own_ref, chirp_ref, matrix_ref, lane_ref, out_ref, tail_ref, work_ref):
     def step(d, carry):
         sign = sign_row()[:1]
         own_cos, own_sin = own_ref[0], own_ref[1]
@@ -648,7 +665,10 @@
         return work_ref[s, plane, pl.ds(row, 8), :]
 
     def store(k, plane, row, value):
-        out_ref[plan.slot(k), plane, pl.ds(row, 8), :] = value
+        if plane == 2:
+            tail_ref[plan.slot(k), 0, pl.ds(row, 8), :] = value
+        else:
+            out_ref[plan.slot(k), plane, pl.ds(row, 8), :] = value
 
     across(plan.count, plan.keep // 8, load, store)
 
@@ -669,7 +689,7 @@
     def store(k, plane, row, value):
         out_ref[k, plane, pl.ds(row, 8), :] = value
 
-    across(plan.count, plan.each // 8, load, store)
+    across_planes(plan.count, plan.each // 8, load, store, x_ref.shape[1])
 
 
 def f32(*shape):
@@ -684,7 +704,7 @@
     return (math.pi / length) * (index * index % (2 * length)).astype(jnp.float32)
 
 
-def pack_kernel(plan, real_ref, imag_ref, kerr_ref, down_ref, along_ref, out_ref):
+def pack_kernel(plan, real_ref, imag_ref, kerr_ref, down_ref, along_ref, out_ref, tail_ref):
     size = 16
     pairs = plan.row_count // 2
 
@@ -704,11 +724,11 @@
             even, odd = 2 * pair, 2 * pair + 1
             out_ref[even, 0, rows, :] = real_a
             out_ref[even, 1, rows, :] = imag_a
-            out_ref[even, 2, rows, :] = jnp.where(low, real_b, swap(imag_b))
+            tail_ref[even, 0, rows, :] = jnp.where(low, real_b, swap(imag_b))
             turned = swap(real_c)
             out_ref[odd, 0, rows, :] = jnp.where(low, swap(real_b), turned)
             out_ref[odd, 1, rows, :] = jnp.where(low, swap(imag_b), swap(imag_c))
-            out_ref[odd, 2, rows, :] = jnp.where(low, turned, imag_c)
+            tail_ref[odd, 0, rows, :] = jnp.where(low, turned, imag_c)
         return carry
 
     lax.fori_loop(0, real_ref.shape[0] // size, step, 0)
@@ -720,15 +740,15 @@
     tile = pl.BlockSpec((rows, cols_here), lambda i: (i, 0))
     return pl.pallas_call(
         functools.partial(pack_kernel, plan),
-        out_shape=f32(plan.row_count, 3, rows_here, LANES),
+        out_shape=(f32(plan.row_count, 2, rows_here, LANES), f32(plan.row_count, 1, rows_here, LANES)),
         grid=(plan.col_count,),
         in_specs=[tile, tile, tile, pl.BlockSpec((rows, LANES), lambda i: (i, 0)), pl.BlockSpec((1, cols_here), lambda i: (0, 0))],
-        out_specs=pl.BlockSpec((plan.row_count, 3, rows, LANES), lambda i: (0, 0, i, 0)),
+        out_specs=tuple(pl.BlockSpec((plan.row_count, planes, rows, LANES), lambda i: (0, 0, i, 0)) for planes in (2, 1)),
         compiler_params=pltpu.CompilerParams(vmem_limit_bytes=40 * 1024 * 1024),
     )(field_real, field_imag, kerr_map, jnp.broadcast_to(down[:, None], (rows_here, LANES)), along[None, :])
 
 
-def unpack_kernel(plan, field_ref, real_ref, imag_ref):
+def unpack_kernel(plan, field_ref, tail_ref, real_ref, imag_ref):
     size = 16
 
     def step(at, carry):
@@ -736,7 +756,7 @@
         low = lax.broadcasted_iota(jnp.int32, (size, LANES), 1) < LANES // 2
         for pair in range(plan.row_count // 2):
             even, odd = 2 * pair, 2 * pair + 1
-            tails = field_ref[even, 0, 2, rows, :], field_ref[odd, 0, 2, rows, :]
+            tails = tail_ref[even, 0, 0, rows, :], tail_ref[odd, 0, 0, rows, :]
             for plane, out_ref in enumerate((real_ref, imag_ref)):
                 own = tails[0] if plane == 0 else swap(tails[0])
                 last = swap(tails[1]) if plane == 0 else tails[1]
@@ -750,16 +770,16 @@
     lax.fori_loop(0, real_ref.shape[0] // size, step, 0)
 
 
-def unpack_field(plan, field, rows_here, cols_here):
+def unpack_field(plan, field, tail, rows_here, cols_here):
     tile = pl.BlockSpec((plan.each, cols_here), lambda i: (i, 0))
     return pl.pallas_call(
         functools.partial(unpack_kernel, plan),
         out_shape=(f32(rows_here, cols_here), f32(rows_here, cols_here)),
         grid=(plan.col_count,),
-        in_specs=[pl.BlockSpec((plan.row_count, 1, 3, plan.each, LANES), lambda i: (0, i, 0, 0, 0))],
+        in_specs=[pl.BlockSpec((plan.row_count, 1, planes, plan.each, LANES), lambda i: (0, i, 0, 0, 0)) for planes in (2, 1)],
         out_specs=(tile, tile),
         compiler_params=pltpu.CompilerParams(vmem_limit_bytes=40 * 1024 * 1024),
-    )(field)
+    )(field, tail)
 
 
 def spread(plan, part, col_at):
@@ -786,10 +806,11 @@
     phase_one = kerr_map * (field_real * field_real + field_imag * field_imag)
     down = lax.dynamic_slice(theta, (row_at * rows_here,), (rows_here,))
     along = lax.dynamic_slice(theta, (col_at * cols_here,), (cols_here,))
-    packed_field = pack_field(plan, field_real, field_imag, kerr_map, down, along)
-    field = lax.all_to_all(packed_field, "rows", split_axis=0, concat_axis=0, tiled=True)
-    kerr = spread(plan, kerr_map.reshape(plan.col_count, each, cols_here), col_at)
-    field, kerr = lax.optimization_barrier((field, kerr))
+    main, tail = pack_field(plan, field_real, field_imag, kerr_map, down, along)
+    tail = lax.all_to_all(tail, "rows", split_axis=0, concat_axis=0, tiled=True)
+    main, tail, kerr_here = lax.optimization_barrier((main, tail, kerr_map))
+    main = lax.all_to_all(main, "rows", split_axis=0, concat_axis=0, tiled=True)
+    kerr = spread(plan, kerr_here.reshape(plan.col_count, each, cols_here), col_at)
     kerr = jnp.transpose(kerr, (0, 2, 1)).reshape(length, each)
     kerr = jnp.stack([kerr[:, :LANES], jnp.concatenate([kerr[:, LANES:], kerr[:, LANES:]], axis=-1)])
 
@@ -813,17 +834,24 @@
     def exchange(part):
         return lax.all_to_all(part, both_axes, split_axis=0, concat_axis=0, tiled=True)
 
-    field = kernel_call(
-        functools.partial(first_kernel, plan), f32(count, 3, each, LANES),
-        (field, plan.tall, plan.column_twist), [scratch(count, 3, each, LANES)],
-    )
-    field = exchange(field)
-    field, mask = lax.optimization_barrier((field, mask))
+    def first(part):
+        return kernel_call(
+            functools.partial(first_kernel, plan), f32(count, part.shape[1], each, LANES),
+            (part, plan.tall, plan.column_twist), [scratch(count, part.shape[1], each, LANES)], 40000,
+        )
+
+    tail = first(tail)
+    main, tail, kerr = lax.optimization_barrier((main, tail, kerr))
+    tail = exchange(tail)
+    main = first(main)
+    main, tail, mask = lax.optimization_barrier((main, tail, mask))
+    main = exchange(main)
+    main, mask = lax.optimization_barrier((main, mask))
     mask = lax.all_to_all(mask, both_axes, split_axis=0, concat_axis=0, tiled=True)
     field, phase_two = kernel_call(
         functools.partial(second_kernel, plan),
         (f32(count, 3, keep, LANES), f32(2, length, LANES)),
-        (field, kerr, theta_wide, own_theta, plan.flip, plan.tall_cut, plan.lane_twist, plan.column_twist),
+        (main, tail, kerr, theta_wide, own_theta, plan.flip, plan.tall_cut, plan.lane_twist, plan.column_twist),
         [scratch(count, 3, each, LANES), scratch(3, length, LANES)],
     )
     field, mask = lax.optimization_barrier((field, mask))
@@ -838,21 +866,32 @@
     )
     field = exchange(field)
     field = kernel_call(
-        functools.partial(fourth_kernel, plan), f32(count, 3, keep, LANES),
+        functools.partial(fourth_kernel, plan), (f32(count, 2, keep, LANES), f32(count, 1, keep, LANES)),
         (field, mask, own_chirp, plan.far_chirp, plan.square, plan.lane_twist), [scratch(count, 3, keep, LANES)],
     )
-    field = exchange(field)
-    field = kernel_call(
-        functools.partial(fifth_kernel, plan), f32(count, 3, each, LANES),
-        (field, plan.tall_back, plan.column_twist), [scratch(count, 3, each, LANES)],
-    )
+    main, tail = field
+    tail = exchange(tail)
+    main, tail = lax.optimization_barrier((main, tail))
+    field = exchange(main), tail
     phase = jnp.concatenate([phase_two[0], phase_two[1][:, :LANES // 2]], axis=-1)
     phase = jnp.transpose(phase.reshape(plan.col_count, cols_here, each), (0, 2, 1))
-    field, phase = lax.optimization_barrier((field, phase))
-    field = field.reshape(plan.row_count, plan.col_count, 3, each, LANES)
+
+    def last(part):
+        part = kernel_call(
+            functools.partial(fifth_kernel, plan), f32(count, part.shape[1], each, LANES),
+            (part, plan.tall_back, plan.column_twist), [scratch(count, part.shape[1], each, LANES)], 40000,
+        )
+        return part.reshape(plan.row_count, plan.col_count, part.shape[1], each, LANES)
+
+    main, tail = field
+    tail = last(tail)
+    main, tail, phase = lax.optimization_barrier((main, tail, phase))
     phase = spread(plan, phase, col_at)
-    field = lax.all_to_all(field, "rows", split_axis=0, concat_axis=0, tiled=True)
-    out_real, out_imag = unpack_field(plan, field, rows_here, cols_here)
+    tail = lax.all_to_all(tail, "rows", split_axis=0, concat_axis=0, tiled=True)
+    main = last(main)
+    main, tail = lax.optimization_barrier((main, tail))
+    main = lax.all_to_all(main, "rows", split_axis=0, concat_axis=0, tiled=True)
+    out_real, out_imag = unpack_field(plan, main, tail, rows_here, cols_here)
     return (out_real, out_imag, phase_one + phase.reshape(rows_here, cols_here))
 
 

time: 1180 us -> 1200 us (1.017)
  waiting for transfers between devices: 607 us -> 401 us
  blocking collectives: 152 us -> 353 us
  Pallas kernels: 259 us -> 280 us
    all_to_all x3, waiting for transfers between devices: 405 us -> 176 us  [exchange(): lax.all_to_all(part, both_axes, split_axis=0, concat_axis=0, tiled=True)]
    all_to_all x1 -> x3, blocking collectives: 152 us -> 353 us  [exchange(): lax.all_to_all(part, both_axes, split_axis=0, concat_axis=0, tiled=True)]
    all_to_all x2 -> x4, waiting for transfers between devices: 0.01 us -> 58.5 us  [the longest x2 58.5 us: fast_device(): tail = lax.all_to_all(tail, 'rows', split_axis=0, concat_axis=0, tiled=True)]
    ppermute x6, waiting for transfers between devices: 202 us -> 167 us  [spread(): lax.ppermute(block, 'cols', [(z, (z + shift) % count) for z in range(coun...]
    pallas_call x5 -> x7, Pallas kernels: 236 us -> 255 us  [kernel_call(): pl.pallas_call(body, out_shape=outs, in_specs=whole(len(inputs)), out_spe...]
  transfers between devices with their start and end apart: 12 -> 14, of which waited for: 7 -> 8; matrix products, arithmetic and copies ran while one was open for 8% -> 8% of each run, Pallas kernels for 8% -> 16%
where the time goes in v4:
time: 1200 us; the launch traced here: 1190 us
  waiting for transfers between devices  401 us (33%)
  blocking collectives  353 us (29%)
  Pallas kernels  280 us (23%)
  local copies, waits for them, and re-layouts  84.6 us (7%)
  starting transfers between devices  46.1 us (4%)
  other arithmetic  29 us (2%)
    all_to_all x3, blocking collectives, exchange(): lax.all_to_all(part, both_axes, split_axis=0, concat_axis=0, tiled=True)  353 us
    pallas_call x7, Pallas kernels, kernel_call(): pl.pallas_call(body, out_shape=outs, in_specs=whole(len(inputs)), out_spe...  255 us
    all_to_all x3, waiting for transfers between devices, exchange(): lax.all_to_all(part, both_axes, split_axis=0, concat_axis=0, tiled=True)  176 us
    ppermute x6, waiting for transfers between devices, spread(): lax.ppermute(block, 'cols', [(z, (z + shift) % count) for z in range(coun...  167 us
    all_to_all x2, waiting for transfers between devices, fast_device(): tail = lax.all_to_all(tail, 'rows', split_axis=0, concat_axis=0, tiled=True)  58.5 us
    unnamed x38, local copies, waits for them, and re-layouts  27.4 us
  transfers between devices with their start and end apart: 14, of which 8 were waited for; matrix products, arithmetic and copies ran while one was open for 8% of the time, Pallas kernels for 16%

profile of v4, /device:TPU:0, one launch (start us, length us, event | category | flops | bytes accessed | tf_op | source)
XLA Modules:
  0.0 1194.8 jit_solution(827868733950907429)
XLA Ops:
  5.7 14.5 %shard_map.157 = (f32[8,2,768,128]{3,2,1,0:T(8,128)}, f32[8,1,768,128]{3,2,1,0:T(8,128)}) custom-call(f32[768,1536]{1,0:T(8,128)S(1)} %copy-done, f32[768,1536]{1,0:T(8,128)S(1)} %copy-done.1, f32[768,1536]{1,0:T(8,128)} %kerr_ref.1, f32[768,128]{1,0:T(8,128)S(1)} %broadcast_in_dim.8.down_ref, f32[1,1536]{1,0:T(1,128)S(1)} %broadcast_in_dim.9.along_ref), custom_call_target="tpu_custom_call" | custom-call | tf_op jit(solution)/shard_map/pallas_call | solution.py:741
  20.2 5.2 all-to-all-start
  25.4 37.8 %all-to-all-done.x_ref = f32[8,1,768,128]{3,2,1,0:T(8,128)S(1)} async-done(((f32[8,1,768,128]{3,2,1,0:T(8,128)}), f32[8,1,768,128]{3,2,1,0:T(8,128)S(1)}, u32[]{:S(2)}, u32[]{:S(2)}) %all-to-all-start) | async-done | bytes 3145760 | tf_op jit(solution)/shard_map/all_to_all | solution.py:810
  77.7 27.6 %shard_map.158 = f32[32,1,192,128]{3,2,1,0:T(8,128)} custom-call(f32[8,1,768,128]{3,2,1,0:T(8,128)} %copy-done.4, bf16[2,384,192]{2,1,0:T(8,128)(2,1)} %constant.125.clone.matrix_ref, f32[192,64]{1,0:T(8,128)} %constant.126.clone.twist_ref.column_ref), custom_call_target="tpu_custom_call" | custom-call | flops 40000000000 | bytes 10000000 | tf_op jit(solution)/shard_map/pallas_call | solution.py:467
  105.4 65.0 %collective-permute-done.1 = f32[1,192,1536]{2,1,0:T(8,128)} collective-permute-done((f32[1,192,1536]{2,1,0:T(8,128)}, f32[1,192,1536]{2,1,0:T(8,128)}, u32[]{:S(2)}, u32[]{:S(2)}) %collective-permute-start.1) | collective-permute-done | bytes 1179680 | tf_op jit(solution)/shard_map/ppermute | solution.py:791
  181.2 6.2 copy.34
  213.5 24.0 %shard_map.159 = f32[32,2,192,128]{3,2,1,0:T(8,128)} custom-call(f32[8,2,768,128]{3,2,1,0:T(8,128)} %all-to-all-done.1.x_ref, bf16[2,384,192]{2,1,0:T(8,128)(2,1)} %constant.125.clone.matrix_ref, f32[192,64]{1,0:T(8,128)} %constant.126.clone.twist_ref.column_ref), custom_call_target="tpu_custom_call" | custom-call | flops 40000000000 | bytes 10000000 | tf_op jit(solution)/shard_map/pallas_call | solution.py:467
  237.5 32.5 %all-to-all-done.2.tail_ref = f32[32,1,192,128]{3,2,1,0:T(8,128)} async-done(((f32[32,1,192,128]{3,2,1,0:T(8,128)}), f32[32,1,192,128]{3,2,1,0:T(8,128)}, u32[]{:S(2)}, u32[]{:S(2)}) %all-to-all-start.2) | async-done | bytes 3145760 | tf_op jit(solution)/shard_map/all_to_all | solution.py:835
  270.0 142.3 %all_to_all.55.x_ref = f32[32,2,192,128]{3,2,1,0:T(8,128)} all-to-all(f32[32,2,192,128]{3,2,1,0:T(8,128)} %shard_map.159), channel_id=1, replica_groups=mesh['rows'=8,'cols'=4] {'rows','cols'}, dimensions={0} | all-to-all | bytes 12582912 | tf_op jit(solution)/shard_map/all_to_all | solution.py:835
  424.8 96.0 %shard_map.160 = (f32[32,3,136,128]{3,2,1,0:T(8,128)}, f32[2,6144,128]{2,1,0:T(8,128)}) custom-call(f32[32,2,192,128]{3,2,1,0:T(8,128)} %all_to_all.55.x_ref, f32[32,1,192,128]{3,2,1,0:T(8,128)} %all-to-all-done.2.tail_ref, f32[2,6144,128]{2,1,0:T(8,128)} %pad_maximum_fusion.kerr_ref, f32[6144,128]{1,0:T(8,128)} %broadcast_in_dim.10.theta_ref, ...), custom_call_target="tpu_custom_call" | custom-call | tf_op jit(solution)/shard_map/pallas_call | solution.py:467
  520.8 152.2 %all_to_all.56.x_ref = f32[32,3,136,128]{3,2,1,0:T(8,128)} all-to-all(f32[32,3,136,128]{3,2,1,0:T(8,128)} %get-tuple-element.45), channel_id=1, replica_groups=mesh['rows'=8,'cols'=4] {'rows','cols'}, dimensions={0} | all-to-all | bytes 13369344 | tf_op jit(solution)/shard_map/all_to_all | solution.py:835
  673.0 30.8 %shard_map.161 = f32[32,304,128]{2,1,0:T(8,128)} custom-call(f32[32,3,136,128]{3,2,1,0:T(8,128)} %all_to_all.56.x_ref, bf16[2,272,384]{2,1,0:T(8,128)(2,1)} %constant.130.clone.matrix_ref, f32[32,4,128]{2,1,0:T(4,128)} %constant.129.clone.lane_ref), custom_call_target="tpu_custom_call" | custom-call | tf_op jit(solution)/shard_map/pallas_call | solution.py:467
  708.0 6.4 copy.38
  731.6 85.2 %all-to-all-done.6.x_ref = f32[32,304,128]{2,1,0:T(8,128)} async-done(((f32[32,304,128]{2,1,0:T(8,128)}), f32[32,304,128]{2,1,0:T(8,128)}, u32[]{:S(2)}, u32[]{:S(2)}) %all-to-all-start.6) | async-done | bytes 4980768 | tf_op jit(solution)/shard_map/all_to_all | solution.py:835
  817.5 34.9 %shard_map.162 = (f32[32,2,136,128]{3,2,1,0:T(8,128)}, f32[32,1,136,128]{3,2,1,0:T(8,128)}) custom-call(f32[32,304,128]{2,1,0:T(8,128)} %all-to-all-done.6.x_ref, f32[32,2,136,128]{3,2,1,0:T(8,128)} %pad_maximum_fusion.1.mask_ref, f32[2,136,128]{2,1,0:T(8,128)} %broadcast_in_dim.11.own_ref, f32[32,4,128]{2,1,0:T(4,128)} %constant.131.clone.chirp_ref, ...), custom_call_target="tpu_custom_call" | custom-call | tf_op jit(solution)/shard_map/pallas_call | solution.py:467
  852.5 58.9 %all_to_all.57.x_ref = f32[32,1,136,128]{3,2,1,0:T(8,128)} all-to-all(f32[32,1,136,128]{3,2,1,0:T(8,128)} %get-tuple-element.48), channel_id=1, replica_groups=mesh['rows'=8,'cols'=4] {'rows','cols'}, dimensions={0} | all-to-all | bytes 4456448 | tf_op jit(solution)/shard_map/all_to_all | solution.py:835
  930.4 24.4 %shard_map.163 = f32[32,1,192,128]{3,2,1,0:T(8,128)} custom-call(f32[32,1,136,128]{3,2,1,0:T(8,128)} %all_to_all.57.x_ref, bf16[2,384,136]{2,1,0:T(8,128)(2,1)} %constant.133.clone.matrix_ref, f32[192,64]{1,0:T(8,128)} %constant.126.clone.twist_ref.column_ref), custom_call_target="tpu_custom_call" | custom-call | flops 40000000000 | bytes 10000000 | tf_op jit(solution)/shard_map/pallas_call | solution.py:467
  954.8 57.8 %all-to-all-done.8.x_ref = f32[32,2,136,128]{3,2,1,0:T(8,128)} async-done(((f32[32,2,136,128]{3,2,1,0:T(8,128)}), f32[32,2,136,128]{3,2,1,0:T(8,128)}, u32[]{:S(2)}, u32[]{:S(2)}) %all-to-all-start.8) | async-done | bytes 4456480 | tf_op jit(solution)/shard_map/all_to_all | solution.py:835
  1017.1 17.5 %shard_map.164 = f32[32,2,192,128]{3,2,1,0:T(8,128)} custom-call(f32[32,2,136,128]{3,2,1,0:T(8,128)} %all-to-all-done.8.x_ref, bf16[2,384,136]{2,1,0:T(8,128)(2,1)} %constant.133.clone.matrix_ref, f32[192,64]{1,0:T(8,128)} %constant.126.clone.twist_ref.column_ref), custom_call_target="tpu_custom_call" | custom-call | flops 40000000000 | bytes 10000000 | tf_op jit(solution)/shard_map/pallas_call | solution.py:467
  1034.6 20.6 %all-to-all-done.9.tail_ref = f32[8,4,1,192,128]{4,3,2,1,0:T(8,128)} async-done(((f32[8,4,1,192,128]{4,3,2,1,0:T(8,128)}), f32[8,4,1,192,128]{4,3,2,1,0:T(8,128)}, u32[]{:S(2)}, u32[]{:S(2)}) %all-to-all-start.9) | async-done | bytes 3145760 | tf_op jit(solution)/shard_map/all_to_all | solution.py:890
  1067.1 24.9 %collective-permute-done.3 = f32[1,192,1536]{2,1,0:T(8,128)S(1)} collective-permute-done((f32[1,192,1536]{2,1,0:T(8,128)S(1)}, f32[1,192,1536]{2,1,0:T(8,128)S(1)}, u32[]{:S(2)}, u32[]{:S(2)}) %collective-permute-start.3) | collective-permute-done | bytes 1179680 | tf_op jit(solution)/shard_map/ppermute | solution.py:791
  1092.1 76.9 %collective-permute-done.4 = f32[1,192,1536]{2,1,0:T(8,128)S(1)} collective-permute-done((f32[1,192,1536]{2,1,0:T(8,128)S(1)}, f32[1,192,1536]{2,1,0:T(8,128)S(1)}, u32[]{:S(2)}, u32[]{:S(2)}) %collective-permute-start.4) | collective-permute-done | bytes 1179680 | tf_op jit(solution)/shard_map/ppermute | solution.py:791
  1176.6 8.2 bitcast_add_fusion
  1184.8 10.0 shard_map.165
  (96 shorter events, 133.7 us)
Async XLA Ops:
  1.0 2.3 copy-start
  3.3 2.3 copy-start.1
  20.2 43.0 %all-to-all-start = ((f32[8,1,768,128]{3,2,1,0:T(8,128)}), f32[8,1,768,128]{3,2,1,0:T(8,128)S(1)}, u32[]{:S(2)}, u32[]{:S(2)}) async-start(f32[8,1,768,128]{3,2,1,0:T(8,128)} %get-tuple-element.32), calls=%async_computation | async-start | bytes 6291456 | tf_op jit(solution)/shard_map/all_to_all | solution.py:810
  63.3 5.0 copy-start.4
  68.3 37.0 %collective-permute-start = (f32[1,192,1536]{2,1,0:T(8,128)}, f32[1,192,1536]{2,1,0:T(8,128)S(1)}, u32[]{:S(2)}, u32[]{:S(2)}) collective-permute-start(f32[1,192,1536]{2,1,0:T(8,128)} %get-tuple-element.70), channel_id=1, source_target_pairs={{0,3},{1,0},{2,1},{3,2},{4,7},{5,4},{6,5},{7,6},{8,11},{9,8},{10,9... | collective-permute-start | bytes 3538952 | tf_op jit(solution)/shard_map/ppermute | solution.py:791
  71.9 98.5 %collective-permute-start.1 = (f32[1,192,1536]{2,1,0:T(8,128)}, f32[1,192,1536]{2,1,0:T(8,128)}, u32[]{:S(2)}, u32[]{:S(2)}) collective-permute-start(f32[1,192,1536]{2,1,0:T(8,128)} %get-tuple-element.69), channel_id=1, source_target_pairs={{0,2},{1,3},{2,0},{3,1},{4,6},{5,7},{6,4},{7,5},{8,10},{9,11},{10,... | collective-permute-start | bytes 3538952 | tf_op jit(solution)/shard_map/ppermute | solution.py:791
  71.9 99.9 %collective-permute-start.2 = (f32[1,192,1536]{2,1,0:T(8,128)}, f32[1,192,1536]{2,1,0:T(8,128)}, u32[]{:S(2)}, u32[]{:S(2)}) collective-permute-start(f32[1,192,1536]{2,1,0:T(8,128)} %get-tuple-element.68), channel_id=1, source_target_pairs={{0,1},{1,2},{2,3},{3,0},{4,5},{5,6},{6,7},{7,4},{8,9},{9,10},{10,1... | collective-permute-start | bytes 3538952 | tf_op jit(solution)/shard_map/ppermute | solution.py:791
  72.9 122.3 %all-to-all-start.1 = ((f32[8,2,768,128]{3,2,1,0:T(8,128)}), f32[8,2,768,128]{3,2,1,0:T(8,128)}, u32[]{:S(2)}, u32[]{:S(2)}) async-start(f32[8,2,768,128]{3,2,1,0:T(8,128)} %get-tuple-element.33), calls=%async_computation.1 | async-start | bytes 12582912 | tf_op jit(solution)/shard_map/all_to_all | solution.py:812
  187.4 3.7 copy-start.2
  195.2 74.8 %all-to-all-start.2 = ((f32[32,1,192,128]{3,2,1,0:T(8,128)}), f32[32,1,192,128]{3,2,1,0:T(8,128)}, u32[]{:S(2)}, u32[]{:S(2)}) async-start(f32[32,1,192,128]{3,2,1,0:T(8,128)} %shard_map.158), calls=%async_computation.2 | async-start | bytes 6291456 | tf_op jit(solution)/shard_map/all_to_all | solution.py:835
  270.0 142.3 %copy-start.3 = (f32[32,136,192]{2,0,1:T(8,128)S(1)}, f32[32,136,192]{2,0,1:T(8,128)}, u32[]{:S(2)}) copy-start(f32[32,136,192]{2,0,1:T(8,128)} %fusion) | copy-start | bytes 10027012
  416.9 103.9 %all-to-all-start.4 = ((f32[32,136,192]{2,1,0:T(8,128)}), f32[32,136,192]{2,1,0:T(8,128)}, u32[]{:S(2)}, u32[]{:S(2)}) async-start(f32[32,136,192]{2,1,0:T(8,128)} %copy.37), calls=%async_computation.4 | async-start | bytes 8912896 | tf_op jit(solution)/shard_map/all_to_all | solution.py:850
  703.9 4.1 copy-start.5
  703.9 112.9 %all-to-all-start.6 = ((f32[32,304,128]{2,1,0:T(8,128)}), f32[32,304,128]{2,1,0:T(8,128)}, u32[]{:S(2)}, u32[]{:S(2)}) async-start(f32[32,304,128]{2,1,0:T(8,128)} %shard_map.161), calls=%async_computation.6 | async-start | bytes 9961472 | tf_op jit(solution)/shard_map/all_to_all | solution.py:835
  911.3 101.3 %all-to-all-start.8 = ((f32[32,2,136,128]{3,2,1,0:T(8,128)}), f32[32,2,136,128]{3,2,1,0:T(8,128)}, u32[]{:S(2)}, u32[]{:S(2)}) async-start(f32[32,2,136,128]{3,2,1,0:T(8,128)} %get-tuple-element.49), calls=%async_computation.8 | async-start | bytes 8912896 | tf_op jit(solution)/shard_map/all_to_all | solution.py:835
  1012.6 42.6 %all-to-all-start.9 = ((f32[8,4,1,192,128]{4,3,2,1,0:T(8,128)}), f32[8,4,1,192,128]{4,3,2,1,0:T(8,128)}, u32[]{:S(2)}, u32[]{:S(2)}) async-start(f32[8,4,1,192,128]{4,3,2,1,0:T(8,128)} %bitcast.54), calls=%async_computation.9 | async-start | bytes 6291456 | tf_op jit(solution)/shard_map/all_to_all | solution.py:890
  1055.2 129.6 %all-to-all-start.10 = ((f32[8,4,2,192,128]{4,3,2,1,0:T(8,128)}), f32[8,4,2,192,128]{4,3,2,1,0:T(8,128)}, u32[]{:S(2)}, u32[]{:S(2)}) async-start(f32[8,4,2,192,128]{4,3,2,1,0:T(8,128)} %bitcast.53), calls=%async_computation.10 | async-start | bytes 12582912 | tf_op jit(solution)/shard_map/all_to_all | solution.py:893
  1062.2 29.8 %collective-permute-start.3 = (f32[1,192,1536]{2,1,0:T(8,128)S(1)}, f32[1,192,1536]{2,1,0:T(8,128)S(1)}, u32[]{:S(2)}, u32[]{:S(2)}) collective-permute-start(f32[1,192,1536]{2,1,0:T(8,128)S(1)} %get-tuple-element.65), channel_id=1, source_target_pairs={{0,3},{1,0},{2,1},{3,2},{4,7},{5,4},{6,5},{7,6},{8,11},{9,8},{10,9... | collective-permute-start | bytes 3538952 | tf_op jit(solution)/shard_map/ppermute | solution.py:791
  1063.6 105.4 %collective-permute-start.4 = (f32[1,192,1536]{2,1,0:T(8,128)S(1)}, f32[1,192,1536]{2,1,0:T(8,128)S(1)}, u32[]{:S(2)}, u32[]{:S(2)}) collective-permute-start(f32[1,192,1536]{2,1,0:T(8,128)S(1)} %get-tuple-element.64), channel_id=1, source_target_pairs={{0,2},{1,3},{2,0},{3,1},{4,6},{5,7},{6,4},{7,5},{8,10},{9,11},{10,... | collective-permute-start | bytes 3538952 | tf_op jit(solution)/shard_map/ppermute | solution.py:791
  1067.0 102.1 %collective-permute-start.5 = (f32[1,192,1536]{2,1,0:T(8,128)S(1)}, f32[1,192,1536]{2,1,0:T(8,128)S(1)}, u32[]{:S(2)}, u32[]{:S(2)}) collective-permute-start(f32[1,192,1536]{2,1,0:T(8,128)S(1)} %get-tuple-element.63), channel_id=1, source_target_pairs={{0,1},{1,2},{2,3},{3,0},{4,5},{5,6},{6,7},{7,4},{8,9},{9,10},{10,1... | collective-permute-start | bytes 3538952 | tf_op jit(solution)/shard_map/ppermute | solution.py:791
  1170.7 4.5 slice-start
  1170.7 5.5 slice-start.2
  1172.4 4.0 slice-start.1
  1172.4 4.2 slice-start.3
